TPU v7x, 512 devices: a whole 4x8x8 slice. The times are simulated.
512 devices in a mesh: strip: 128 (over x, z_lo, y), branch: 4 (over z_hi, core).
Axes of the slice: x: 4, y: 8, z: 8 (z_hi: 2, z_lo: 4; z = z_hi * 4 + z_lo), core: 2. Of those that a mesh axis runs over, the one named last changes fastest.
Arguments:
- features: bfloat16 [1024, 192, 512], P('strip'), may hold values from -6 to 6
- cotangent: bfloat16 [1024, 192, 256], P('strip', None, 'branch'), may hold values from -6 to 6
- depth_weight: bfloat16 [4, 9, 512], P('branch'), may hold values from -2 to 2
- point_weight: bfloat16 [4, 512, 256], P('branch'), may hold values from -0.25 to 0.25
- joining_weight: bfloat16 [1024, 256], P('branch'), may hold values from -0.25 to 0.25
- branch_mask: int32 [4], replicated, may hold values from 0 to 1, as said below
Outputs:
- output: bfloat16 [1024, 192, 256], P('strip', None, 'branch')
- joining_grad: float32 [1024, 256], P('branch')
- point_grad: float32 [4, 512, 256], P('branch')
- depth_grad: float32 [4, 9, 512], P('branch')
Inputs may be any that keep to these rules, and one draw needn't show every extreme that they name: `branch_mask`: 1 marks an active branch; at least one branch is active and at least one is not.
All inputs are finite; a program needn't handle non-finite values.
Results may differ from a plain program's by a relative error of at most 0.014.
Values may be sent and summed in bfloat16 or wider, within the bound.
A program may use at most 64 MiB of HBM per device.

v0:
```python
import math

import jax
import jax.numpy as jnp
from jax import lax
from jax.sharding import PartitionSpec as P

DILATION_STEP = 6


tanh_coef = 0.7978845608
cubic_coef = 0.044715
slope_coef = 0.134145


def shifted(value, axis, steps):
    count = lax.axis_size(axis)
    leading, last = (max(0, -steps), min(count, count - steps))
    return lax.ppermute(value, axis, [(source, source + steps) for source in range(leading, last)])


def gelu_tanh(values):
    inner = jnp.tanh(tanh_coef * (values + cubic_coef * values * values * values))
    return 0.5 * values * (1.0 + inner)


def gelu_slope(values):
    inner = jnp.tanh(tanh_coef * (values + cubic_coef * values * values * values))
    return 0.5 * (1.0 + inner) + 0.5 * values * (1.0 - inner * inner) * tanh_coef * (
        1.0 + slope_coef * values * values
    )


def contract_rows(left, right):
    return lax.dot_general(
        left, right, (((0,), (0,)), ((), ())), preferred_element_type=jnp.float32
    )


def contract_cols(left, right):
    return lax.dot_general(
        left, right, (((1,), (1,)), ((), ())), preferred_element_type=jnp.float32
    )


def tap_piece(padded, border_rows, dilation_rate, tap_index, row_count, col_count, chan_count):
    row_start = border_rows + (tap_index // 3 - 1) * dilation_rate
    col_start = border_rows + (tap_index % 3 - 1) * dilation_rate
    return lax.dynamic_slice(padded, (row_start, col_start, 0), (row_count, col_count, chan_count))


def strip_from(features, offset):
    return shifted(features, "strip", offset)


def per_device(features, cotangent, depth_weight, point_weight, joining_weight, branch_mask):
    row_count, col_count, chan_count = features.shape
    pixel_count = row_count * col_count
    strip_count = lax.axis_size("strip")
    branch_total = lax.axis_size("branch")
    local_branch = lax.axis_index("branch")
    dilation_rate = (local_branch + 1) * DILATION_STEP
    border_rows = branch_total * DILATION_STEP
    hop_count = (border_rows + row_count - 1) // row_count
    pixel_scale = 1.0 / math.sqrt(pixel_count * strip_count)
    active = jnp.sum(
        jnp.where(jnp.arange(branch_mask.shape[0]) == local_branch, branch_mask, 0)
    ).astype(jnp.float32)
    above = [strip_from(features, hop) for hop in range(hop_count, 0, -1)]
    below = [strip_from(features, -hop) for hop in range(1, hop_count + 1)]
    stacked = jnp.concatenate(above + [features] + below, 0)
    first_row = hop_count * row_count - border_rows
    padded = stacked
    padded = jnp.pad(padded, ((0, 0), (border_rows, border_rows), (0, 0)))
    kernel = depth_weight[0].astype(jnp.float32)
    summed = jnp.zeros(features.shape, jnp.float32)
    for tap_index in range(9):
        piece = tap_piece(
            padded, border_rows, dilation_rate, tap_index, row_count, col_count, chan_count
        )
        summed = summed + piece.astype(jnp.float32) * kernel[tap_index]
    dw_out = summed.astype(jnp.bfloat16).reshape(pixel_count, chan_count)
    pre_act = jnp.dot(dw_out, point_weight[0], preferred_element_type=jnp.float32)
    branch_out = (gelu_tanh(pre_act) * active).astype(jnp.bfloat16)
    own_width = cotangent.shape[2]
    partial_sum = jnp.dot(branch_out, joining_weight, preferred_element_type=jnp.float32)
    joined_sum = lax.psum_scatter(
        partial_sum.astype(jnp.bfloat16), "branch", scatter_dimension=1, tiled=True
    ).astype(jnp.float32)
    output = gelu_tanh(joined_sum).astype(jnp.bfloat16).reshape(row_count, col_count, own_width)
    grad_joined = (
        cotangent.reshape(pixel_count, own_width).astype(jnp.float32) * gelu_slope(joined_sum)
    ).astype(jnp.bfloat16)
    full_grad = lax.all_gather(grad_joined, "branch", axis=1, tiled=True)
    joining_part = contract_rows(branch_out, full_grad) * pixel_scale
    grad_branch = contract_cols(full_grad, joining_weight) * active
    grad_pre = (grad_branch * gelu_slope(pre_act)).astype(jnp.bfloat16)
    point_part = contract_rows(dw_out, grad_pre) * pixel_scale
    depthwise_gradient = contract_cols(grad_pre, point_weight[0]).reshape(
        row_count, col_count, chan_count
    )
    tap_sums = []
    for tap_index in range(9):
        piece = tap_piece(
            padded, border_rows, dilation_rate, tap_index, row_count, col_count, chan_count
        )
        tap_sums.append(
            jnp.sum(depthwise_gradient * piece.astype(jnp.float32), axis=(0, 1)) * pixel_scale
        )
    depth_part = jnp.stack(tap_sums)
    joining_total, point_total, depth_total = lax.psum(
        (joining_part, point_part, depth_part), "strip"
    )
    return (output, joining_total, point_total[None], depth_total[None])


def solution(mesh):
    placed = (
        P("strip", None, None),
        P("strip", None, "branch"),
        P("branch", None, None),
        P("branch", None, None),
        P("branch", None),
        P(),
    )
    return jax.shard_map(
        per_device,
        mesh=mesh,
        in_specs=placed,
        out_specs=(
            P("strip", None, "branch"),
            P("branch", None),
            P("branch", None, None),
            P("branch", None, None),
        ),
        check_vma=False,
    )
```

profile of v0, /device:TPU:8, one launch (start us, length us, event | category | flops | bytes accessed | tf_op | source)
XLA Modules:
  0.0 1683.8 jit_solution(2562978151916074131)
XLA Ops:
  7.2 0.0 copy-start
  7.2 0.0 reduce-scatter.2.cloned.1.call-start
  7.2 8.0 collective-permute-start
  15.2 1.6 collective-permute-start.1
  16.9 2.9 collective-permute-start.2
  19.8 4.1 collective-permute-start.3
  23.9 1.3 collective-permute-start.4
  25.2 91.3 %collective-permute-done = bf16[8,192,512]{2,1,0:T(8,128)(2,1)} collective-permute-done((bf16[8,192,512]{2,1,0:T(8,128)(2,1)}, bf16[8,192,512]{2,1,0:T(8,128)(2,1)}, u32[]{:S(2)}, u32[]{:S(2)}) %collective-permute-start) | collective-permute-done | bytes 1572896 | tf_op jit(solution)/shard_map/ppermute | solution.py:19
  116.5 1.3 collective-permute-start.5
  117.8 1.3 fusion.41
  119.7 1.0 fusion.42
  120.7 1.5 constant_dynamic-update-slice_fusion.6
  122.2 59.8 %collective-permute-done.1 = bf16[8,192,512]{2,1,0:T(8,128)(2,1)S(1)} collective-permute-done((bf16[8,192,512]{2,1,0:T(8,128)(2,1)}, bf16[8,192,512]{2,1,0:T(8,128)(2,1)S(1)}, u32[]{:S(2)}, u32[]{:S(2)}) %collective-permute-start.1) | collective-permute-done | bytes 1572896 | tf_op jit(solution)/shard_map/ppermute | solution.py:19
  182.1 0.2 constant_dynamic-update-slice_fusion.5
  182.3 0.0 copy-start.2
  182.3 34.5 %collective-permute-done.2 = bf16[8,192,512]{2,1,0:T(8,128)(2,1)} collective-permute-done((bf16[8,192,512]{2,1,0:T(8,128)(2,1)}, bf16[8,192,512]{2,1,0:T(8,128)(2,1)}, u32[]{:S(2)}, u32[]{:S(2)}) %collective-permute-start.2) | collective-permute-done | bytes 1572896 | tf_op jit(solution)/shard_map/ppermute | solution.py:19
  216.7 1.5 constant_dynamic-update-slice_fusion.4
  218.2 0.0 copy-done.2
  218.2 0.2 constant_dynamic-update-slice_fusion.3
  218.4 0.0 collective-permute-done.3
  218.4 1.5 constant_dynamic-update-slice_fusion.2
  219.9 0.0 collective-permute-done.4
  219.9 0.2 constant_dynamic-update-slice_fusion.1
  220.1 0.0 collective-permute-done.5
  220.1 1.5 constant_dynamic-update-slice_fusion
  221.6 0.0 copy-start.1
  221.7 5.1 fusion.8
  226.8 0.0 copy-done.1
  226.8 0.0 copy-done
  226.8 0.0 copy-start.6
  226.8 0.6 fusion.39
  227.4 0.0 copy-start.3
  227.4 1.1 copy-done.3
  228.5 0.0 copy-done.6
  228.5 1.7 convolution_convert_fusion
  230.3 0.0 reduce-scatter.2.cloned.1.call-update
  230.3 0.0 all-reduce.4.cloned.1.call-start
  230.4 1.9 copy.10
  232.3 2.0 reshape.130
  234.2 59.1 %reduce-scatter.2.cloned.1.call-done = bf16[1536,64]{0,1:T(8,128)(2,1)} async-done(((bf16[1536,256]{0,1:T(8,128)(2,1)}), bf16[1536,64]{0,1:T(8,128)(2,1)}) %reduce-scatter.2.cloned.1.call-update) | async-done | bytes 196624 | tf_op jit(solution)/shard_map/reduce_scatter | solution.py:87
  293.4 0.0 copy-start.4
  293.4 2.1 fusion.33
  295.5 15.4 all_gather.3
  310.9 0.0 copy-done.4
  310.9 1.2 fusion.19
  312.1 0.0 copy-start.7
  312.1 1.4 convolution_multiply_fusion.2
  313.5 0.0 copy-done.7
  313.5 1.4 fusion.25
  314.9 0.0 copy-start.5
  314.9 8.8 fusion.17
  323.7 0.0 all-reduce.4.cloned.1.call-update
  323.8 0.1 stack.2
  323.9 0.0 copy-done.5
  323.9 0.2 reshape.129
  324.1 0.8 copy.11
  324.9 716.6 %psum.23 = f32[1,9,512]{2,0,1:T(1,128)} all-reduce(f32[1,9,512]{2,0,1:T(1,128)S(1)} %broadcast_in_dim.12), channel_id=1, replica_groups=mesh['strip'=128,'branch'=4] {'strip'}, use_global_device_ids=true, to_apply=%region_13.14 | all-reduce | flops 4608 | bytes 36864 | tf_op jit(solution)/shard_map/psum | solution.py:111
  1041.4 632.0 %all-reduce.4.cloned.1.call-done = (f32[256,256]{1,0:T(8,128)}, f32[1,512,256]{2,1,0:T(8,128)}) async-done(((f32[256,256]{1,0:T(8,128)}, f32[1,512,256]{2,1,0:T(8,128)}), (f32[256,256]{1,0:T(8,128)}, f32[1,512,256]{2,1,0:T(8,128)})) %all-reduce.4.cloned.1.call-update) | async-done | bytes 786448 | tf_op jit(solution)/shard_map/psum | solution.py:111
  1673.5 1.7 copy.20
  1675.1 1.9 copy.21
  (6 shorter events, 0.0 us)
Async XLA Ops:
  7.2 219.6 %copy-start = (bf16[1,512,256]{2,1,0:T(8,128)(2,1)S(1)}, bf16[1,512,256]{2,1,0:T(8,128)(2,1)}, u32[]{:S(2)}) copy-start(bf16[1,512,256]{2,1,0:T(8,128)(2,1)} %param.9) | copy-start | bytes 786436
  7.2 286.2 %reduce-scatter.2.cloned.1.call-start = ((), (), s32[]{:S(2)}) async-start(), calls=%async_computation.1 | async-start | bytes 983040 | tf_op jit(solution)/shard_map/reduce_scatter | solution.py:87
  7.2 109.3 %collective-permute-start = (bf16[8,192,512]{2,1,0:T(8,128)(2,1)}, bf16[8,192,512]{2,1,0:T(8,128)(2,1)}, u32[]{:S(2)}, u32[]{:S(2)}) collective-permute-start(bf16[8,192,512]{2,1,0:T(8,128)(2,1)} %param.6), channel_id=1, source_target_pairs={{0,12},{4,16},{8,20},{12,24},{16,28},{20,32},{24,36},{28,40},{32,4... | collective-permute-start | bytes 4718600 | tf_op jit(solution)/shard_map/ppermute | solution.py:19
  15.2 166.8 %collective-permute-start.1 = (bf16[8,192,512]{2,1,0:T(8,128)(2,1)}, bf16[8,192,512]{2,1,0:T(8,128)(2,1)S(1)}, u32[]{:S(2)}, u32[]{:S(2)}) collective-permute-start(bf16[8,192,512]{2,1,0:T(8,128)(2,1)} %param.6), channel_id=1, source_target_pairs={{0,8},{4,12},{8,16},{12,20},{16,24},{20,28},{24,32},{28,36},{32,40... | collective-permute-start | bytes 4718600 | tf_op jit(solution)/shard_map/ppermute | solution.py:19
  16.9 199.8 %collective-permute-start.2 = (bf16[8,192,512]{2,1,0:T(8,128)(2,1)}, bf16[8,192,512]{2,1,0:T(8,128)(2,1)}, u32[]{:S(2)}, u32[]{:S(2)}) collective-permute-start(bf16[8,192,512]{2,1,0:T(8,128)(2,1)} %param.6), channel_id=1, source_target_pairs={{0,4},{4,8},{8,12},{12,16},{16,20},{20,24},{24,28},{28,32},{32,36}... | collective-permute-start | bytes 4718600 | tf_op jit(solution)/shard_map/ppermute | solution.py:19
  19.8 198.7 %collective-permute-start.3 = (bf16[8,192,512]{2,1,0:T(8,128)(2,1)}, bf16[8,192,512]{2,1,0:T(8,128)(2,1)}, u32[]{:S(2)}, u32[]{:S(2)}) collective-permute-start(bf16[8,192,512]{2,1,0:T(8,128)(2,1)} %param.6), channel_id=1, source_target_pairs={{4,0},{8,4},{12,8},{16,12},{20,16},{24,20},{28,24},{32,28},{36,32}... | collective-permute-start | bytes 4718600 | tf_op jit(solution)/shard_map/ppermute | solution.py:19
  23.9 196.1 %collective-permute-start.4 = (bf16[8,192,512]{2,1,0:T(8,128)(2,1)}, bf16[8,192,512]{2,1,0:T(8,128)(2,1)S(1)}, u32[]{:S(2)}, u32[]{:S(2)}) collective-permute-start(bf16[8,192,512]{2,1,0:T(8,128)(2,1)} %param.6), channel_id=1, source_target_pairs={{8,0},{12,4},{16,8},{20,12},{24,16},{28,20},{32,24},{36,28},{40,32... | collective-permute-start | bytes 4718600 | tf_op jit(solution)/shard_map/ppermute | solution.py:19
  116.5 103.6 %collective-permute-start.5 = (bf16[8,192,512]{2,1,0:T(8,128)(2,1)}, bf16[8,192,512]{2,1,0:T(8,128)(2,1)}, u32[]{:S(2)}, u32[]{:S(2)}) collective-permute-start(bf16[8,192,512]{2,1,0:T(8,128)(2,1)} %param.6), channel_id=1, source_target_pairs={{12,0},{16,4},{20,8},{24,12},{28,16},{32,20},{36,24},{40,28},{44,3... | collective-permute-start | bytes 4718600 | tf_op jit(solution)/shard_map/ppermute | solution.py:19
  182.3 36.0 %copy-start.2 = (bf16[8,192,512]{2,1,0:T(8,128)(2,1)S(1)}, bf16[8,192,512]{2,1,0:T(8,128)(2,1)}, u32[]{:S(2)}) copy-start(bf16[8,192,512]{2,1,0:T(8,128)(2,1)} %param.6) | copy-start | bytes 4718596
  221.6 5.2 copy-start.1
  226.8 1.7 copy-start.6
  227.4 1.1 copy-start.3
  230.3 1443.1 %all-reduce.4.cloned.1.call-start = ((), (), s32[]{:S(2)}) async-start(), calls=%async_computation.2 | async-start | bytes 1572864 | tf_op jit(solution)/shard_map/psum | solution.py:111
  293.4 17.5 %copy-start.4 = (f32[1536,256]{1,0:T(8,128)S(1)}, f32[1536,256]{1,0:T(8,128)}, u32[]{:S(2)}) copy-start(f32[1536,256]{1,0:T(8,128)} %copy-done.3) | copy-start | bytes 4718596
  312.1 1.4 copy-start.7
  314.9 8.9 copy-start.5
Sparse Core Ops, SparseCore 0:
  230.4 62.9 reduce-scatter.1
  323.9 1349.5 all-reduce.3
where the time goes:
time: 1680 us
  waiting for transfers between devices  877 us (52%)
  blocking collectives  732 us (44%)
  starting transfers between devices  19.3 us (1%)
  local copies, waits for them, and re-layouts  17.2 us (1%)
    psum x1, blocking collectives, per_device(): lax.psum((joining_part, point_part, depth_part), 'strip')  717 us
    psum x1, waiting for transfers between devices, per_device(): lax.psum((joining_part, point_part, depth_part), 'strip')  632 us
    ppermute x6, waiting for transfers between devices, shifted(): lax.ppermute(value, axis, [(source, source + steps) for source in range(l...  186 us
    reduce_scatter x1, waiting for transfers between devices, per_device(): lax.psum_scatter(partial_sum.astype(jnp.bfloat16), 'branch', scatter_dime...  59.1 us
  transfers between devices with their start and end apart: 8, of which 5 were waited for; matrix products, arithmetic and copies ran while one was open for 1% of the time, Pallas kernels for 0%

commit v1 on v0

v1 whole, which is shorter than its diff:
```python
import functools
import math

import jax
import jax.numpy as jnp
from jax import lax
from jax.experimental import pallas as pl
from jax.experimental.pallas import tpu as pltpu
from jax.sharding import PartitionSpec as P

DILATION_STEP = 6
HOPS = 3
MESH = pl.DeviceIdType.MESH

tanh_coef = 0.7978845608
cubic_coef = 0.044715
slope_coef = 0.134145


def gelu_tanh(values):
    inner = jnp.tanh(tanh_coef * (values + cubic_coef * values * values * values))
    return 0.5 * values * (1.0 + inner)


def gelu_slope(values):
    inner = jnp.tanh(tanh_coef * (values + cubic_coef * values * values * values))
    return 0.5 * (1.0 + inner) + 0.5 * values * (1.0 - inner * inner) * tanh_coef * (
        1.0 + slope_coef * values * values
    )


def contract_rows(left, right):
    return lax.dot_general(
        left, right, (((0,), (0,)), ((), ())), preferred_element_type=jnp.float32
    )


def contract_cols(left, right):
    return lax.dot_general(
        left, right, (((1,), (1,)), ((), ())), preferred_element_type=jnp.float32
    )


def tap_piece(padded, border_rows, dilation_rate, tap_index, row_count, col_count, chan_count):
    row_start = border_rows + (tap_index // 3 - 1) * dilation_rate
    col_start = border_rows + (tap_index % 3 - 1) * dilation_rate
    return lax.dynamic_slice(padded, (row_start, col_start, 0), (row_count, col_count, chan_count))


def greet(barrier, partners):
    for partner in partners:
        pl.semaphore_signal(barrier, inc=1, device_id=partner, device_id_type=MESH)
    pl.semaphore_wait(barrier, len(partners))


def strip_layout(strip_count):
    if strip_count == 128:
        return 4, 4, 8
    return {4: (2, 1, 2), 8: (2, 2, 2), 2: (2, 1, 1)}[strip_count]


def halo_kernel(strip_count, feat, ext, zeros, own_sem, zero_sem, send, recv, pass_send, pass_recv):
    rows = feat.shape[0]
    half = rows // 2
    strip = lax.axis_index("strip")
    branch = lax.axis_index("branch")
    core = lax.rem(branch, 2)
    sibling = branch + 1 - 2 * core
    after = lax.rem(strip + 1, strip_count)
    before = lax.rem(strip + strip_count - 1, strip_count)
    barrier = pltpu.get_barrier_semaphore()
    greet(barrier, [(after, branch), (before, branch), (strip, sibling)])

    centre = HOPS * rows
    own = pltpu.make_async_copy(feat, ext.at[pl.ds(centre, rows)], own_sem)
    own.start()

    def exists(offset):
        place = strip + offset
        return jnp.logical_and(place >= 0, place < strip_count)

    def place_of(offset, line, side):
        return centre + offset * rows + half * side + line

    def link_copy(way, step, line):
        at = 0 if way > 0 else 1
        target = after if way > 0 else before
        if step == 0:
            source = feat.at[pl.ds(half * core + line, 1)]
        else:
            source = ext.at[pl.ds(place_of(-way * step, line, core), 1)]
        return pltpu.make_async_remote_copy(
            src_ref=source,
            dst_ref=ext.at[pl.ds(place_of(-way * (step + 1), line, core), 1)],
            send_sem=send.at[at, step, line],
            recv_sem=recv.at[at, step, line],
            device_id=(target, branch),
            device_id_type=MESH,
        )

    def pass_copy(way, step, line, side):
        at = 0 if way > 0 else 1
        rows_at = ext.at[pl.ds(place_of(-way * (step + 1), line, side), 1)]
        return pltpu.make_async_remote_copy(
            src_ref=rows_at,
            dst_ref=rows_at,
            send_sem=pass_send.at[at, step, line],
            recv_sem=pass_recv.at[at, step, line],
            device_id=(strip, sibling),
            device_id_type=MESH,
        )

    every = [(step, line, way) for step in range(HOPS) for line in range(half) for way in (1, -1)]

    for step, line, way in every:
        if step == 0:

            @pl.when(exists(way))
            def _():
                link_copy(way, step, line).start()

    for offset in range(1, HOPS + 1):
        for way in (1, -1):

            @pl.when(jnp.logical_not(exists(offset * way)))
            def _():
                zeros[...] = jnp.zeros_like(zeros)
                fill = pltpu.make_async_copy(
                    zeros, ext.at[pl.ds(centre + offset * way * rows, rows)], zero_sem
                )
                fill.start()
                fill.wait()

    for step, line, way in every:

        @pl.when(exists(-way * (step + 1)))
        def _():
            link_copy(way, step, line).wait_recv()
            pass_copy(way, step, line, core).start()

        if step + 1 < HOPS:

            @pl.when(jnp.logical_and(exists(-way * (step + 1)), exists(way)))
            def _():
                link_copy(way, step + 1, line).start()

    for step, line, way in every:

        @pl.when(jnp.logical_and(exists(-way * step), exists(way)))
        def _():
            link_copy(way, step, line).wait_send()

        @pl.when(exists(-way * (step + 1)))
        def _():
            pass_copy(way, step, line, core).wait_send()
            pass_copy(way, step, line, 1 - core).wait_recv()

    own.wait()


def halo(features, strip_count):
    rows, cols, chans = features.shape
    half = rows // 2
    return pl.pallas_call(
        functools.partial(halo_kernel, strip_count),
        name="halo_rows",
        out_shape=jax.ShapeDtypeStruct(((2 * HOPS + 1) * rows, cols, chans), features.dtype),
        in_specs=[pl.BlockSpec(memory_space=pl.ANY)],
        out_specs=pl.BlockSpec(memory_space=pl.ANY),
        scratch_shapes=[
            pltpu.VMEM((rows, cols, chans), features.dtype),
            pltpu.SemaphoreType.DMA,
            pltpu.SemaphoreType.DMA,
            pltpu.SemaphoreType.DMA((2, HOPS, half)),
            pltpu.SemaphoreType.DMA((2, HOPS, half)),
            pltpu.SemaphoreType.DMA((2, HOPS, half)),
            pltpu.SemaphoreType.DMA((2, HOPS, half)),
        ],
        compiler_params=pltpu.CompilerParams(collective_id=0, has_side_effects=True),
    )(features)


CHUNKS = 3


def swap_halves(low, high):
    lane = lax.broadcasted_iota(jnp.int32, low.shape, 1)
    left = lane < 64
    return (
        jnp.where(left, low, pltpu.roll(high, 64, 1)),
        jnp.where(left, pltpu.roll(low, 64, 1), high),
    )


def join_kernel(
    branch_out, weight, cot, out, full_grad, blocks, total, near, far, away, grads,
    near_send, near_recv, far_send, far_recv, gfar_send, gfar_recv, gnear_send, gnear_recv,
):
    strip = lax.axis_index("strip")
    branch = lax.axis_index("branch")
    core = lax.rem(branch, 2)
    layer = branch // 2
    sibling = (strip, branch + 1 - 2 * core)
    across = (strip, branch + 2 - 4 * layer)
    barrier = pltpu.get_barrier_semaphore()
    greet(barrier, [sibling, across])
    pixels = branch_out.shape[0] // 2
    size = pixels // CHUNKS

    def span(chunk):
        return pl.ds(chunk * size, size)

    def remote(source, target, send_sem, recv_sem, device):
        return pltpu.make_async_remote_copy(
            src_ref=source, dst_ref=target, send_sem=send_sem, recv_sem=recv_sem,
            device_id=device, device_id_type=MESH,
        )

    def near_copy(chunk, side):
        return remote(
            blocks.at[2 * side + 1 - core, span(chunk)], near.at[side, span(chunk)],
            near_send.at[chunk, side], near_recv.at[chunk, side], sibling,
        )

    def far_copy(chunk):
        return remote(
            away.at[span(chunk)], far.at[span(chunk)], far_send.at[chunk], far_recv.at[chunk], across
        )

    def grad_far(chunk):
        spot = grads.at[branch, span(chunk)]
        return remote(spot, spot, gfar_send.at[chunk], gfar_recv.at[chunk], across)

    def grad_near(chunk, which, block):
        spot = grads.at[block, span(chunk)]
        return remote(spot, spot, gnear_send.at[chunk, which], gnear_recv.at[chunk, which], sibling)

    for chunk in range(CHUNKS):
        low = jnp.dot(branch_out[chunk * size:(chunk + 1) * size, :], weight[...], preferred_element_type=jnp.float32)
        high = jnp.dot(
            branch_out[pixels + chunk * size:pixels + (chunk + 1) * size, :], weight[...],
            preferred_element_type=jnp.float32,
        )
        for pair in range(2):
            first, second = swap_halves(
                low[:, 128 * pair:128 * (pair + 1)], high[:, 128 * pair:128 * (pair + 1)]
            )
            blocks[2 * pair, span(chunk), :] = first.astype(jnp.bfloat16)
            blocks[2 * pair + 1, span(chunk), :] = second.astype(jnp.bfloat16)
        for side in range(2):
            near_copy(chunk, side).start()

    for chunk in range(CHUNKS):
        for side in range(2):
            near_copy(chunk, side).wait_recv()
        there = 1 - layer
        away[span(chunk), :] = (
            blocks[2 * there + core, span(chunk), :].astype(jnp.float32)
            + near[there, span(chunk), :].astype(jnp.float32)
        ).astype(jnp.bfloat16)
        far_copy(chunk).start()
        total[span(chunk), :] = blocks[branch, span(chunk), :].astype(jnp.float32) + near[
            layer, span(chunk), :
        ].astype(jnp.float32)

    for chunk in range(CHUNKS):
        far_copy(chunk).wait_recv()
        joined = total[span(chunk), :] + far[span(chunk), :].astype(jnp.float32)
        inner = jnp.tanh(tanh_coef * (joined + cubic_coef * joined * joined * joined))
        slope = 0.5 * (1.0 + inner) + 0.5 * joined * (1.0 - inner * inner) * tanh_coef * (
            1.0 + slope_coef * joined * joined
        )
        grads[branch, span(chunk), :] = (cot[span(chunk), :].astype(jnp.float32) * slope).astype(
            jnp.bfloat16
        )
        grad_far(chunk).start()
        grad_near(chunk, 0, branch).start()
        out[span(chunk), :] = (0.5 * joined * (1.0 + inner)).astype(out.dtype)

    other = branch + 2 - 4 * layer
    beside = branch + 1 - 2 * core
    beside_other = other + 1 - 2 * core
    for chunk in range(CHUNKS):
        grad_far(chunk).wait_recv()
        grad_near(chunk, 1, other).start()
    for chunk in range(CHUNKS):
        grad_near(chunk, 0, beside).wait_recv()
        grad_near(chunk, 1, beside_other).wait_recv()
        for pair in range(2):
            low, high = swap_halves(
                grads[2 * pair, span(chunk), :].astype(jnp.float32),
                grads[2 * pair + 1, span(chunk), :].astype(jnp.float32),
            )
            full_grad[chunk * size:(chunk + 1) * size, 128 * pair:128 * (pair + 1)] = low.astype(jnp.bfloat16)
            full_grad[pixels + chunk * size:pixels + (chunk + 1) * size, 128 * pair:128 * (pair + 1)] = high.astype(
                jnp.bfloat16
            )

    for chunk in range(CHUNKS):
        for side in range(2):
            near_copy(chunk, side).wait_send()
        far_copy(chunk).wait_send()
        grad_far(chunk).wait_send()
        grad_near(chunk, 0, branch).wait_send()
        grad_near(chunk, 1, other).wait_send()


def join(branch_out, weight, cotangent):
    pixels, chans = branch_out.shape
    pixels = pixels // 2
    packed = jnp.concatenate([cotangent[:pixels], cotangent[pixels:]], axis=1)
    vmem = pl.BlockSpec(memory_space=pltpu.VMEM)
    out, full_grad = pl.pallas_call(
        join_kernel,
        name="joined_sum",
        out_shape=(
            jax.ShapeDtypeStruct((pixels, 128), jnp.bfloat16),
            jax.ShapeDtypeStruct((2 * pixels, chans), jnp.bfloat16),
        ),
        in_specs=[vmem] * 3,
        out_specs=(vmem, vmem),
        scratch_shapes=[
            pltpu.VMEM((4, pixels, 128), jnp.bfloat16),
            pltpu.VMEM((pixels, 128), jnp.float32),
            pltpu.VMEM((2, pixels, 128), jnp.bfloat16),
            pltpu.VMEM((pixels, 128), jnp.bfloat16),
            pltpu.VMEM((pixels, 128), jnp.bfloat16),
            pltpu.VMEM((4, pixels, 128), jnp.bfloat16),
            pltpu.SemaphoreType.DMA((CHUNKS, 2)),
            pltpu.SemaphoreType.DMA((CHUNKS, 2)),
            pltpu.SemaphoreType.DMA((CHUNKS,)),
            pltpu.SemaphoreType.DMA((CHUNKS,)),
            pltpu.SemaphoreType.DMA((CHUNKS,)),
            pltpu.SemaphoreType.DMA((CHUNKS,)),
            pltpu.SemaphoreType.DMA((CHUNKS, 2)),
            pltpu.SemaphoreType.DMA((CHUNKS, 2)),
        ],
        compiler_params=pltpu.CompilerParams(
            collective_id=1, has_side_effects=True, vmem_limit_bytes=32 << 20
        ),
    )(branch_out, weight, packed)
    output = jnp.concatenate([out[:, :64], out[:, 64:]], axis=0)
    return output, full_grad


def total_kernel(
    layout, piece, stored, scale, joining, point, depth, joining_out, point_out, depth_out,
    mine, from_x, from_y, from_z, gathered,
    x_send, x_recv, y_send, y_recv, z_send, z_recv, gy_send, gy_recv, gx_send, gx_recv,
):
    nx, nz, ny = layout
    strip = lax.axis_index("strip")
    branch = lax.axis_index("branch")
    y = lax.rem(strip, ny)
    z = lax.rem(strip // ny, nz)
    x = strip // (ny * nz)

    def x_peer(step):
        other = lax.rem(x + step, nx)
        return other, ((other * nz + z) * ny + y, branch)

    def y_peer(step):
        other = lax.rem(y + step, ny)
        return other, ((x * nz + z) * ny + other, branch)

    def z_peer(step):
        other = lax.rem(z + step, nz)
        return other, ((x * nz + other) * ny + y, branch)

    def remote(source, target, send_sem, recv_sem, device):
        return pltpu.make_async_remote_copy(
            src_ref=source, dst_ref=target, send_sem=send_sem, recv_sem=recv_sem,
            device_id=device, device_id_type=MESH,
        )

    barrier = pltpu.get_barrier_semaphore()
    greet(
        barrier,
        [x_peer(k)[1] for k in range(1, nx)]
        + [y_peer(k)[1] for k in range(1, ny)]
        + [z_peer(k)[1] for k in range(1, nz)],
    )

    per_half = nx * ny // 2
    pieces = []
    for lane_half in range(2):
        tables = [
            (joining, joining_out, 0, 256, 128 * lane_half),
            (point, point_out, 256, 768, 128 * lane_half),
            (depth, depth_out, 768, 784, 256 * lane_half),
            (depth, depth_out, 784, 800, 256 * lane_half + 128),
        ]
        for index in range(per_half):
            at = lane_half * per_half + index
            start, stop = index * piece, (index + 1) * piece
            for source, target, first, last, lane in tables:
                low, high = max(start, first), min(stop, last)
                if low < high:
                    pieces.append((at // ny, at % ny, low - start, high - start, source, target, low - first, high - first, lane))
            if stop > 800:
                pieces.append((at // ny, at % ny, max(800 - start, 0), piece, None, None, 0, 0, 0))
    for px, py, low, high, source, _, first, last, lane in pieces:
        if source is None:
            mine[px, py, low:high, :] = jnp.zeros((high - low, 128), jnp.float32)
        else:
            mine[px, py, low:high, :] = source[first:last, lane:lane + 128]

    def x_copy(step):
        other, device = x_peer(step)
        return remote(mine.at[other], from_x.at[step - 1], x_send.at[step - 1], x_recv.at[step - 1], device)

    for step in range(1, nx):
        x_copy(step).start()
    for step in range(1, nx):
        x_copy(step).wait_recv()
    summed = mine[x]
    for step in range(1, nx):
        summed = summed + from_x[step - 1]
    from_y[0] = summed

    def y_copy(step):
        other, device = y_peer(step)
        return remote(from_y.at[0, other], from_y.at[1, step - 1], y_send.at[step - 1], y_recv.at[step - 1], device)

    for step in range(1, ny):
        y_copy(step).start()
    for step in range(1, ny):
        y_copy(step).wait_recv()
    summed = from_y[0, y]
    for step in range(1, ny):
        summed = summed + from_y[1, step - 1]
    from_z[z] = summed

    def z_copy(step):
        spot = from_z.at[z]
        return remote(spot, spot, z_send.at[step - 1], z_recv.at[step - 1], z_peer(step)[1])

    for step in range(1, nz):
        z_copy(step).start()
    for step in range(1, nz):
        z_copy(step).wait_recv()
    summed = from_z[0]
    for other in range(1, nz):
        summed = summed + from_z[other]
    gathered[x, y, 0:piece, :] = (summed * scale).astype(jnp.bfloat16)
    if stored > piece:
        gathered[x, y, piece:stored, :] = jnp.zeros((stored - piece, 128), jnp.bfloat16)

    def gy_copy(step):
        spot = gathered.at[x, y]
        return remote(spot, spot, gy_send.at[step - 1], gy_recv.at[step - 1], y_peer(step)[1])

    for step in range(1, ny):
        gy_copy(step).start()
    for step in range(1, ny):
        gy_copy(step).wait_recv()

    def gx_copy(step):
        spot = gathered.at[x]
        return remote(spot, spot, gx_send.at[step - 1], gx_recv.at[step - 1], x_peer(step)[1])

    for step in range(1, nx):
        gx_copy(step).start()
    for step in range(1, nx):
        gx_copy(step).wait_recv()

    for px, py, low, high, source, target, first, last, lane in pieces:
        if source is not None:
            target[first:last, lane:lane + 128] = gathered[px, py, 0:piece, :].astype(jnp.float32)[low:high, :]

    for step in range(1, nx):
        x_copy(step).wait_send()
        gx_copy(step).wait_send()
    for step in range(1, ny):
        y_copy(step).wait_send()
        gy_copy(step).wait_send()
    for step in range(1, nz):
        z_copy(step).wait_send()


def weight_totals(joining, point, depth, scale, strip_count):
    nx, nz, ny = strip_layout(strip_count)
    piece = -(-1600 // (nx * ny) // 8) * 8
    stored = -(-piece // 16) * 16
    vmem = pl.BlockSpec(memory_space=pltpu.VMEM)
    dma = pltpu.SemaphoreType.DMA
    padded = jnp.concatenate([depth, jnp.zeros((16 - depth.shape[0], depth.shape[1]), jnp.float32)], 0)
    shapes = [joining.shape, point.shape, padded.shape]
    a, b, c = pl.pallas_call(
        functools.partial(total_kernel, (nx, nz, ny), piece, stored, scale),
        name="weight_totals",
        out_shape=tuple(jax.ShapeDtypeStruct(shape, jnp.float32) for shape in shapes),
        in_specs=[vmem] * 3,
        out_specs=(vmem,) * 3,
        scratch_shapes=[
            pltpu.VMEM((nx, ny, piece, 128), jnp.float32),
            pltpu.VMEM((max(nx - 1, 1), ny, piece, 128), jnp.float32),
            pltpu.VMEM((2, ny, piece, 128), jnp.float32),
            pltpu.VMEM((nz, piece, 128), jnp.float32),
            pltpu.VMEM((nx, ny, stored, 128), jnp.bfloat16),
            dma((nx,)), dma((nx,)), dma((ny,)), dma((ny,)), dma((nz,)), dma((nz,)),
            dma((ny,)), dma((ny,)), dma((nx,)), dma((nx,)),
        ],
        compiler_params=pltpu.CompilerParams(
            collective_id=2, has_side_effects=True, vmem_limit_bytes=32 << 20
        ),
    )(joining, point, padded)
    return a, b, c[: depth.shape[0]]


def per_device(features, cotangent, depth_weight, point_weight, joining_weight, branch_mask):
    row_count, col_count, chan_count = features.shape
    pixel_count = row_count * col_count
    strip_count = lax.axis_size("strip")
    branch_total = lax.axis_size("branch")
    local_branch = lax.axis_index("branch")
    dilation_rate = (local_branch + 1) * DILATION_STEP
    border_rows = branch_total * DILATION_STEP
    pixel_scale = 1.0 / math.sqrt(pixel_count * strip_count)
    active = jnp.sum(
        jnp.where(jnp.arange(branch_mask.shape[0]) == local_branch, branch_mask, 0)
    ).astype(jnp.float32)
    stacked = halo(features, strip_count)
    padded = jnp.pad(stacked, ((0, 0), (border_rows, border_rows), (0, 0)))
    kernel = depth_weight[0].astype(jnp.float32)
    summed = jnp.zeros(features.shape, jnp.float32)
    for tap_index in range(9):
        piece = tap_piece(
            padded, border_rows, dilation_rate, tap_index, row_count, col_count, chan_count
        )
        summed = summed + piece.astype(jnp.float32) * kernel[tap_index]
    dw_out = summed.astype(jnp.bfloat16).reshape(pixel_count, chan_count)
    pre_act = jnp.dot(dw_out, point_weight[0], preferred_element_type=jnp.float32)
    branch_out = (gelu_tanh(pre_act) * active).astype(jnp.bfloat16)
    own_width = cotangent.shape[2]
    output, full_grad = join(branch_out, joining_weight, cotangent.reshape(pixel_count, own_width))
    output = output.reshape(row_count, col_count, own_width)
    joining_part = contract_rows(branch_out, full_grad)
    grad_branch = contract_cols(full_grad, joining_weight) * active
    grad_pre = (grad_branch * gelu_slope(pre_act)).astype(jnp.bfloat16)
    point_part = contract_rows(dw_out, grad_pre)
    depthwise_gradient = contract_cols(grad_pre, point_weight[0]).reshape(
        row_count, col_count, chan_count
    )
    tap_sums = []
    for tap_index in range(9):
        piece = tap_piece(
            padded, border_rows, dilation_rate, tap_index, row_count, col_count, chan_count
        )
        tap_sums.append(jnp.sum(depthwise_gradient * piece.astype(jnp.float32), axis=(0, 1)))
    depth_part = jnp.stack(tap_sums)
    joining_total, point_total, depth_total = weight_totals(
        joining_part, point_part, depth_part, pixel_scale, strip_count
    )
    return (output, joining_total, point_total[None], depth_total[None])


def solution(mesh):
    placed = (
        P("strip", None, None),
        P("strip", None, "branch"),
        P("branch", None, None),
        P("branch", None, None),
        P("branch", None),
        P(),
    )
    return jax.shard_map(
        per_device,
        mesh=mesh,
        in_specs=placed,
        out_specs=(
            P("strip", None, "branch"),
            P("branch", None),
            P("branch", None, None),
            P("branch", None, None),
        ),
        check_vma=False,
    )
```

time: 1680 us -> 165 us (0.10)
  the two profiles are of different devices: /device:TPU:8 before, /device:TPU:4 now
where the time goes in v1:
time: 165 us
  Pallas kernels  134 us (81%)
  matrix products  12.9 us (8%)
  other arithmetic  10.1 us (6%)
  local copies, waits for them, and re-layouts  6.22 us (4%)
    pallas_call x1, Pallas kernels, halo(): pl.pallas_call(functools.partial(halo_kernel, strip_count), name='halo_ro...  64.8 us
    pallas_call x1, Pallas kernels, weight_totals(): pl.pallas_call(functools.partial(total_kernel, (nx, nz, ny), piece, store...  42.3 us
    pallas_call x1, Pallas kernels, join(): pl.pallas_call(join_kernel, name='joined_sum', out_shape=(jax.ShapeDtypeS...  27.3 us
    dot_general x2, matrix products, contract_cols(): lax.dot_general(left, right, (((1,), (1,)), ((), ())), preferred_element_...  9.93 us
    convert_element_type x1, other arithmetic, per_device(): dw_out = summed.astype(jnp.bfloat16).reshape(pixel_count, chan_count)  8.57 us
    unnamed x16, local copies, waits for them, and re-layouts  4.68 us

profile of v1, /device:TPU:4, one launch (start us, length us, event | category | flops | bytes accessed | tf_op | source)
XLA Modules:
  0.0 165.1 jit_solution(9257785571862512993)
XLA Ops:
  0.6 0.0 copy-start
  0.7 1.3 fusion.29
  2.6 1.0 fusion.32
  3.6 64.8 %halo_rows.1 = bf16[56,192,512]{2,1,0:T(8,128)(2,1)} custom-call(bf16[8,192,512]{2,1,0:T(8,128)(2,1)} %feat.1), custom_call_target="tpu_custom_call" | custom-call | tf_op jit(solution)/shard_map/halo_rows/pallas_call | solution.py:164
  68.4 8.6 %fusion.8 = bf16[8,192,512]{2,1,0:T(8,128)(2,1)S(1)} fusion(f32[512]{0:T(512)S(1)} %bitcast.58, f32[512]{0:T(512)S(1)} %bitcast.57, f32[512]{0:T(512)S(1)} %bitcast.56, f32[512]{0:T(512)S(1)} %bitcast.55, f32[512]{0:T(512)S(1)} %bitcast.54, f32[512]{0:T(512)S(1)} %bitcast.53, f32[512]{0:T(512)S(1)} %bitcast.52, f32[512]{0:T(512)S(1)} %bitcast.51, ...), kind=kLoop, calls=%fused_computation.34 | loop fusion | flops 21233664 | bytes 14174224 | tf_op jit(solution)/shard_map/convert_element_type | solution.py:532
  77.0 0.0 copy-start.2
  77.0 0.0 copy-done
  77.0 0.0 copy-start.4
  77.1 2.0 %multiply_convert_fusion = (bf16[1536,256]{1,0:T(8,128)(2,1)S(1)}, f32[1536,256]{1,0:T(8,128)}) fusion(f32[]{:T(128)S(6)} %convert_element_type.65, bf16[1536,512]{1,0:T(8,128)(2,1)S(1)} %bitcast.45, bf16[1,512,256]{2,1,0:T(8,128)(2,1)S(1)} %copy-done), kind=kOutput, calls=%fused_computation.54 | convolution fusion | flops 406585344 | bytes 4194308 | tf_op jit(solution)/shard_map/dot_general | solution.py:533
  79.0 0.0 copy-done.2
  79.0 0.0 copy-start.1
  79.0 0.0 copy-done.4
  79.0 0.2 copy.11
  79.2 0.2 copy.10
  79.4 0.1 pad_maximum_fusion.1.cot
  79.5 0.4 copy-done.1
  79.9 27.3 %joined_sum.1 = (bf16[768,128]{1,0:T(8,128)(2,1)S(1)}, bf16[1536,256]{1,0:T(8,128)(2,1)S(1)}) custom-call(bf16[1536,256]{1,0:T(8,128)(2,1)S(1)} %get-tuple-element.40.branch_out, bf16[256,256]{1,0:T(8,128)(2,1)S(1)} %copy-done.1, bf16[768,128]{1,0:T(8,128)(2,1)S(1)} %pad_maximum_fusion.1.cot), custom_call_target="tpu_custom_call" | custom-call | tf_op jit(solution)/shard_map/joined_sum/pallas_call | solution.py:313
  107.2 0.1 fusion.31
  107.3 0.1 pad_maximum_fusion
  107.4 0.9 copy.12
  108.3 0.0 copy-start.5
  108.3 0.4 fusion.33.joining
  108.7 1.0 copy-done.5
  109.7 0.0 copy-start.3
  109.7 1.2 fusion.19
  110.9 0.2 copy-done.3
  111.2 0.6 fusion.34.point
  111.8 8.8 %fusion.17 = (f32[512]{0:T(512)S(1)}, f32[512]{0:T(512)S(1)}, f32[512]{0:T(512)S(1)}, f32[512]{0:T(512)S(1)}, f32[512]{0:T(512)S(1)}, /*index=5*/f32[512]{0:T(51...) fusion(s32[]{:T(128)S(6)} %select_n.15, s32[]{:T(128)S(6)} %select_n.14, bf16[56,192,512]{2,1,0:T(8,128)(2,1)} %halo_rows.1, ...), kind=kOutput, calls=%fused_computation.43 | convolution fusion | flops 423882240 | bytes 13649936 | tf_op jit(solution)/shard_map/dot_general | solution.py:39
  120.5 0.1 concatenate.11.depth
  120.6 42.3 %weight_totals.1 = (f32[256,256]{1,0:T(8,128)S(1)}, f32[512,256]{1,0:T(8,128)S(1)}, f32[16,512]{1,0:T(8,128)S(1)}) custom-call(f32[256,256]{1,0:T(8,128)S(1)} %fusion.33.joining, f32[512,256]{1,0:T(8,128)S(1)} %fusion.34.point, f32[16,512]{1,0:T(8,128)S(1)} %concatenate.11.depth), custom_call_target="tpu_custom_call" | custom-call | tf_op jit(solution)/shard_map/weight_totals/pallas_call | solution.py:489
  162.9 0.6 copy.13
  163.6 0.7 copy.16
  164.3 0.8 copy.17
  (3 shorter events, 0.0 us)
Async XLA Ops:
  0.6 76.4 %copy-start = (bf16[1,512,256]{2,1,0:T(8,128)(2,1)S(1)}, bf16[1,512,256]{2,1,0:T(8,128)(2,1)}, u32[]{:S(2)}) copy-start(bf16[1,512,256]{2,1,0:T(8,128)(2,1)} %param.9) | copy-start | bytes 786436
  77.0 2.0 %copy-start.2 = (bf16[8,192,512]{2,1,0:T(8,128)(2,1)}, bf16[8,192,512]{2,1,0:T(8,128)(2,1)S(1)}, u32[]{:S(2)}) copy-start(bf16[8,192,512]{2,1,0:T(8,128)(2,1)S(1)} %fusion.8) | copy-start | bytes 4718596
  77.0 2.0 %copy-start.4 = (bf16[8,192,64]{1,2,0:T(8,128)(2,1)S(1)}, bf16[8,192,64]{1,2,0:T(8,128)(2,1)}, u32[]{:S(2)}) copy-start(bf16[8,192,64]{1,2,0:T(8,128)(2,1)} %param.7) | copy-start | bytes 589828
  79.0 0.9 copy-start.1
  108.3 1.4 copy-start.5
  109.7 1.4 copy-start.3

commit v2 on v1

v2 whole, which is shorter than its diff:
```python
import functools
import math

import jax
import jax.numpy as jnp
from jax import lax
from jax.experimental import pallas as pl
from jax.experimental.pallas import tpu as pltpu
from jax.sharding import PartitionSpec as P

DILATION_STEP = 6
HOPS = 3
MESH = pl.DeviceIdType.MESH

tanh_coef = 0.7978845608
cubic_coef = 0.044715
slope_coef = 0.134145


def contract_rows(left, right):
    return lax.dot_general(
        left, right, (((0,), (0,)), ((), ())), preferred_element_type=jnp.float32
    )


def contract_cols(left, right):
    return lax.dot_general(
        left, right, (((1,), (1,)), ((), ())), preferred_element_type=jnp.float32
    )


def greet(barrier, partners):
    for partner in partners:
        pl.semaphore_signal(barrier, inc=1, device_id=partner, device_id_type=MESH)
    pl.semaphore_wait(barrier, len(partners))


def strip_layout(strip_count):
    if strip_count == 128:
        return 4, 4, 8
    return {4: (2, 1, 2), 8: (2, 2, 2), 2: (2, 1, 1)}[strip_count]


CHUNKS = 4
LOW_ROWS = (2, 3, 0, 1)
HIGH_ROWS = (4, 5, 6, 7)
EDGE = 24


def swap_halves(low, high):
    lane = lax.broadcasted_iota(jnp.int32, low.shape, 1)
    left = lane < 64
    return (
        jnp.where(left, low, pltpu.roll(high, 64, 1)),
        jnp.where(left, pltpu.roll(low, 64, 1), high),
    )


def branch_kernel(
    strip_count, feat, cot, depth_w, point_w, join_w, active, out, join_part, point_part, depth_part,
    ext, taps, dw_out, slope, branch_out, blocks, near, away, far, total, grads, grad_dw,
    own_sem, send, recv, pass_send, pass_recv,
    near_send, near_recv, far_send, far_recv, gfar_send, gfar_recv, gnear_send, gnear_recv,
):
    rows, cols, chans = feat.shape
    half = rows // 2
    tiles = chans // 128
    strip = lax.axis_index("strip")
    branch = lax.axis_index("branch")
    core = lax.rem(branch, 2)
    layer = branch // 2
    rate = (branch + 1) * DILATION_STEP
    beside = branch + 1 - 2 * core
    other = branch + 2 - 4 * layer
    beside_other = other + 1 - 2 * core
    sibling = (strip, beside)
    across = (strip, other)
    after = (lax.rem(strip + 1, strip_count), branch)
    before = (lax.rem(strip + strip_count - 1, strip_count), branch)
    greet(pltpu.get_barrier_semaphore(), [after, before, sibling, across])

    def remote(source, target, send_sem, recv_sem, device):
        return pltpu.make_async_remote_copy(
            src_ref=source, dst_ref=target, send_sem=send_sem, recv_sem=recv_sem,
            device_id=device, device_id_type=MESH,
        )

    centre = HOPS * rows

    def exists(offset):
        place = strip + offset
        return jnp.logical_and(place >= 0, place < strip_count)

    def line_row(line, side):
        return side * HIGH_ROWS[line] + (1 - side) * LOW_ROWS[line]

    def link_copy(way, step, line):
        at = 0 if way > 0 else 1
        row = line_row(line, core)
        if step == 0:
            source = feat.at[pl.ds(row, 1)]
        else:
            source = ext.at[pl.ds(centre - way * step * rows + row, 1)]
        return remote(
            source, ext.at[pl.ds(centre - way * (step + 1) * rows + row, 1)],
            send.at[at, step, line], recv.at[at, step, line], after if way > 0 else before,
        )

    def pass_copy(way, step, line, side):
        at = 0 if way > 0 else 1
        spot = ext.at[pl.ds(centre - way * (step + 1) * rows + line_row(line, side), 1)]
        return remote(spot, spot, pass_send.at[at, step, line], pass_recv.at[at, step, line], sibling)

    ways = (1, -1)
    for line in range(half):
        for way in ways:

            @pl.when(exists(way))
            def _():
                link_copy(way, 0, line).start()

    own = pltpu.make_async_copy(feat, ext.at[pl.ds(centre, rows)], own_sem)
    own.start()

    for offset in range(1, HOPS + 1):
        for way in ways:

            @pl.when(jnp.logical_not(exists(offset * way)))
            def _():
                def fill(row, carry):
                    ext[centre + offset * way * rows + row] = jnp.zeros((cols, chans), ext.dtype)
                    return carry

                lax.fori_loop(0, rows, fill, 0)

    def clear(index, carry):
        for part in range(3):
            for tile in range(tiles):
                taps[index, part, tile, 0:EDGE, :] = jnp.zeros((EDGE, 128), jnp.float32)
                taps[index, part, tile, EDGE + cols:2 * EDGE + cols, :] = jnp.zeros((EDGE, 128), jnp.float32)
        return carry

    lax.fori_loop(0, rows, clear, 0)
    join_part[...] = jnp.zeros_like(join_part)
    point_part[...] = jnp.zeros_like(point_part)
    depth_part[...] = jnp.zeros_like(depth_part)

    def widen(row, part):
        at = centre + row + (part - 1) * rate
        for tile in range(tiles):
            taps[row, part, tile, EDGE:EDGE + cols, :] = ext[at, :, 128 * tile:128 * (tile + 1)].astype(jnp.float32)

    own.wait()

    def widen_own(row, carry):
        widen(row, 1)
        return carry

    lax.fori_loop(0, rows, widen_own, 0)

    def arrive(step, line):
        for way in ways:

            @pl.when(exists(-way * (step + 1)))
            def _():
                link_copy(way, step, line).wait_recv()

            if step + 1 < HOPS:

                @pl.when(jnp.logical_and(exists(-way * (step + 1)), exists(way)))
                def _():
                    link_copy(way, step + 1, line).start()

            @pl.when(exists(-way * (step + 1)))
            def _():
                pass_copy(way, step, line, core).start()

    def passed(step, line):
        for way in ways:

            @pl.when(exists(-way * (step + 1)))
            def _():
                pass_copy(way, step, line, 1 - core).wait_recv()

    def tap_columns(part):
        return pl.ds(EDGE + (part - 1) * rate, cols)

    def near_copy(chunk, side):
        return remote(
            blocks.at[2 * side + 1 - core, chunk], near.at[side, chunk],
            near_send.at[chunk, side], near_recv.at[chunk, side], sibling,
        )

    def far_copy(chunk):
        return remote(away.at[chunk], far.at[chunk], far_send.at[chunk], far_recv.at[chunk], across)

    def grad_far(chunk):
        spot = grads.at[branch, chunk]
        return remote(spot, spot, gfar_send.at[chunk], gfar_recv.at[chunk], across)

    def grad_near(chunk, which, block):
        spot = grads.at[block, chunk]
        return remote(spot, spot, gnear_send.at[chunk, which], gnear_recv.at[chunk, which], sibling)

    def forward(chunk):
        arrive(HOPS - 1, chunk)
        passed(HOPS - 1, chunk)
        for place, row in ((0, LOW_ROWS[chunk]), (1, HIGH_ROWS[chunk])):
            widen(row, 0)
            widen(row, 2)

            def depthwise(tile, carry):
                summed = jnp.zeros((cols, 128), jnp.float32)
                for part in range(9):
                    piece = taps[row, part // 3, tile, tap_columns(part % 3), :]
                    summed = summed + piece * depth_w[tile, part:part + 1, :]
                dw_out[chunk, place * cols:(place + 1) * cols, pl.ds(pl.multiple_of(tile * 128, 128), 128)] = (
                    summed.astype(jnp.bfloat16)
                )
                return carry

            lax.fori_loop(0, tiles, depthwise, 0)
        pre = jnp.dot(dw_out[chunk], point_w[...], preferred_element_type=jnp.float32)
        inner = jnp.tanh(tanh_coef * (pre + cubic_coef * pre * pre * pre))
        slope[chunk] = 0.5 * (1.0 + inner) + 0.5 * pre * (1.0 - inner * inner) * tanh_coef * (
            1.0 + slope_coef * pre * pre
        )
        branch_out[chunk] = (0.5 * pre * (1.0 + inner) * active[...]).astype(jnp.bfloat16)
        part_sum = jnp.dot(branch_out[chunk], join_w[...], preferred_element_type=jnp.float32)
        for pair in range(2):
            lanes = slice(128 * pair, 128 * (pair + 1))
            first, second = swap_halves(part_sum[:cols, lanes], part_sum[cols:, lanes])
            blocks[2 * pair, chunk] = first.astype(jnp.bfloat16)
            blocks[2 * pair + 1, chunk] = second.astype(jnp.bfloat16)
        for side in range(2):
            near_copy(chunk, side).start()

    def pair_sum(chunk):
        for side in range(2):
            near_copy(chunk, side).wait_recv()
        there = 1 - layer
        away[chunk] = (
            blocks[2 * there + core, chunk].astype(jnp.float32) + near[there, chunk].astype(jnp.float32)
        ).astype(jnp.bfloat16)
        far_copy(chunk).start()
        total[chunk] = blocks[branch, chunk].astype(jnp.float32) + near[layer, chunk].astype(jnp.float32)

    def finish_sum(chunk):
        far_copy(chunk).wait_recv()
        joined = total[chunk] + far[chunk].astype(jnp.float32)
        inner = jnp.tanh(tanh_coef * (joined + cubic_coef * joined * joined * joined))
        rise = 0.5 * (1.0 + inner) + 0.5 * joined * (1.0 - inner * inner) * tanh_coef * (
            1.0 + slope_coef * joined * joined
        )
        grads[branch, chunk] = (cot[chunk].astype(jnp.float32) * rise).astype(jnp.bfloat16)
        grad_far(chunk).start()
        grad_near(chunk, 0, branch).start()
        out[chunk] = (0.5 * joined * (1.0 + inner)).astype(out.dtype)

    def hand_on(chunk):
        grad_far(chunk).wait_recv()
        grad_near(chunk, 1, other).start()

    def backward(chunk):
        grad_near(chunk, 0, beside).wait_recv()
        grad_near(chunk, 1, beside_other).wait_recv()
        low_parts, high_parts = [], []
        for pair in range(2):
            low, high = swap_halves(
                grads[2 * pair, chunk].astype(jnp.float32), grads[2 * pair + 1, chunk].astype(jnp.float32)
            )
            low_parts.append(low)
            high_parts.append(high)
        full_grad = jnp.concatenate(
            [jnp.concatenate(low_parts, axis=1), jnp.concatenate(high_parts, axis=1)], axis=0
        ).astype(jnp.bfloat16)
        grad_branch = contract_cols(full_grad, join_w[...]) * active[...]
        grad_pre = (grad_branch * slope[chunk]).astype(jnp.bfloat16)
        grad_dw[...] = contract_cols(grad_pre, point_w[...])
        join_part[...] += contract_rows(branch_out[chunk], full_grad)
        point_part[...] += contract_rows(dw_out[chunk], grad_pre)
        for place, row in ((0, LOW_ROWS[chunk]), (1, HIGH_ROWS[chunk])):

            def depth_sums(tile, carry):
                here = grad_dw[place * cols:(place + 1) * cols, pl.ds(pl.multiple_of(tile * 128, 128), 128)]
                for part in range(9):
                    product = here * taps[row, part // 3, tile, tap_columns(part % 3), :]
                    depth_part[tile, part] += jnp.sum(product.reshape(cols // 8, 8, 128), axis=0)
                return carry

            lax.fori_loop(0, tiles, depth_sums, 0)

    for step in range(HOPS - 1):
        for line in range(half):
            arrive(step, line)
    for step in range(HOPS - 1):
        for line in range(half):
            passed(step, line)

    stages = (forward, pair_sum, finish_sum, hand_on, backward)
    for turn in range(CHUNKS + len(stages) - 1):
        for index, stage in enumerate(stages):
            if 0 <= turn - index < CHUNKS:
                stage(turn - index)

    for step in range(HOPS):
        for line in range(half):
            for way in ways:

                @pl.when(jnp.logical_and(exists(-way * step), exists(way)))
                def _():
                    link_copy(way, step, line).wait_send()

                @pl.when(exists(-way * (step + 1)))
                def _():
                    pass_copy(way, step, line, core).wait_send()

    for chunk in range(CHUNKS):
        for side in range(2):
            near_copy(chunk, side).wait_send()
        far_copy(chunk).wait_send()
        grad_far(chunk).wait_send()
        grad_near(chunk, 0, branch).wait_send()
        grad_near(chunk, 1, other).wait_send()


def branch_step(features, cotangent, depth_weight, point_weight, joining_weight, active, strip_count):
    rows, cols, chans = features.shape
    width = point_weight.shape[1]
    half = rows // 2
    tiles = chans // 128

    def lines(array, order):
        return jnp.concatenate([array[row:row + 1] for row in order], 0)

    packed = jnp.concatenate([lines(cotangent, LOW_ROWS), lines(cotangent, HIGH_ROWS)], axis=2)
    taps_weight = depth_weight.astype(jnp.float32).reshape(9, tiles, 128).transpose(1, 0, 2)
    vmem = pl.BlockSpec(memory_space=pltpu.VMEM)
    dma = pltpu.SemaphoreType.DMA
    low, wide = jnp.bfloat16, jnp.float32
    out, join_part, point_part, depth_part = pl.pallas_call(
        functools.partial(branch_kernel, strip_count),
        name="branch_step",
        out_shape=(
            jax.ShapeDtypeStruct((CHUNKS, cols, 128), low),
            jax.ShapeDtypeStruct((width, width), wide),
            jax.ShapeDtypeStruct((chans, width), wide),
            jax.ShapeDtypeStruct((tiles, 9, 8, 128), wide),
        ),
        in_specs=[pl.BlockSpec(memory_space=pl.ANY)] + [vmem] * 5,
        out_specs=(vmem,) * 4,
        scratch_shapes=[
            pltpu.VMEM(((2 * HOPS + 1) * rows, cols, chans), low),
            pltpu.VMEM((rows, 3, tiles, cols + 2 * EDGE, 128), wide),
            pltpu.VMEM((CHUNKS, 2 * cols, chans), low),
            pltpu.VMEM((CHUNKS, 2 * cols, width), wide),
            pltpu.VMEM((CHUNKS, 2 * cols, width), low),
            pltpu.VMEM((4, CHUNKS, cols, 128), low),
            pltpu.VMEM((2, CHUNKS, cols, 128), low),
            pltpu.VMEM((CHUNKS, cols, 128), low),
            pltpu.VMEM((CHUNKS, cols, 128), low),
            pltpu.VMEM((CHUNKS, cols, 128), wide),
            pltpu.VMEM((4, CHUNKS, cols, 128), low),
            pltpu.VMEM((2 * cols, chans), wide),
            dma,
            dma((2, HOPS, half)), dma((2, HOPS, half)), dma((2, HOPS, half)), dma((2, HOPS, half)),
            dma((CHUNKS, 2)), dma((CHUNKS, 2)), dma((CHUNKS,)), dma((CHUNKS,)),
            dma((CHUNKS,)), dma((CHUNKS,)), dma((CHUNKS, 2)), dma((CHUNKS, 2)),
        ],
        compiler_params=pltpu.CompilerParams(
            collective_id=0, has_side_effects=True, vmem_limit_bytes=52 << 20
        ),
    )(features, packed, taps_weight, point_weight, joining_weight, active)
    by_row = {}
    for chunk in range(CHUNKS):
        by_row[LOW_ROWS[chunk]] = out[chunk:chunk + 1, :, :64]
        by_row[HIGH_ROWS[chunk]] = out[chunk:chunk + 1, :, 64:]
    output = jnp.concatenate([by_row[row] for row in range(rows)], 0)
    return output, join_part, point_part, depth_part


def total_kernel(
    layout, piece, stored, scale, joining, point, depth, joining_out, point_out, depth_out,
    depth_rows, mine, from_x, from_y, from_z, gathered,
    x_send, x_recv, y_send, y_recv, z_send, z_recv, gy_send, gy_recv, gx_send, gx_recv,
):
    nx, nz, ny = layout
    strip = lax.axis_index("strip")
    branch = lax.axis_index("branch")
    y = lax.rem(strip, ny)
    z = lax.rem(strip // ny, nz)
    x = strip // (ny * nz)

    def x_peer(step):
        other = lax.rem(x + step, nx)
        return other, ((other * nz + z) * ny + y, branch)

    def y_peer(step):
        other = lax.rem(y + step, ny)
        return other, ((x * nz + z) * ny + other, branch)

    def z_peer(step):
        other = lax.rem(z + step, nz)
        return other, ((x * nz + other) * ny + y, branch)

    def remote(source, target, send_sem, recv_sem, device):
        return pltpu.make_async_remote_copy(
            src_ref=source, dst_ref=target, send_sem=send_sem, recv_sem=recv_sem,
            device_id=device, device_id_type=MESH,
        )

    barrier = pltpu.get_barrier_semaphore()
    greet(
        barrier,
        [x_peer(k)[1] for k in range(1, nx)]
        + [y_peer(k)[1] for k in range(1, ny)]
        + [z_peer(k)[1] for k in range(1, nz)],
    )

    depth_rows[...] = jnp.zeros_like(depth_rows)
    for tile in range(depth.shape[0]):
        for part in range(depth.shape[1]):
            depth_rows[part:part + 1, 128 * tile:128 * (tile + 1)] = jnp.sum(depth[tile, part], axis=0, keepdims=True)

    per_half = nx * ny // 2
    pieces = []
    for lane_half in range(2):
        tables = [
            (joining, joining_out, 0, 256, 128 * lane_half),
            (point, point_out, 256, 768, 128 * lane_half),
            (depth_rows, depth_out, 768, 784, 256 * lane_half),
            (depth_rows, depth_out, 784, 800, 256 * lane_half + 128),
        ]
        for index in range(per_half):
            at = lane_half * per_half + index
            start, stop = index * piece, (index + 1) * piece
            for source, target, first, last, lane in tables:
                low, high = max(start, first), min(stop, last)
                if low < high:
                    pieces.append((at // ny, at % ny, low - start, high - start, source, target, low - first, high - first, lane))
            if stop > 800:
                pieces.append((at // ny, at % ny, max(800 - start, 0), piece, None, None, 0, 0, 0))
    for px, py, low, high, source, _, first, last, lane in pieces:
        if source is None:
            mine[px, py, low:high, :] = jnp.zeros((high - low, 128), jnp.float32)
        else:
            mine[px, py, low:high, :] = source[first:last, lane:lane + 128]

    def x_copy(step):
        other, device = x_peer(step)
        return remote(mine.at[other], from_x.at[step - 1], x_send.at[step - 1], x_recv.at[step - 1], device)

    for step in range(1, nx):
        x_copy(step).start()
    for step in range(1, nx):
        x_copy(step).wait_recv()
    summed = mine[x]
    for step in range(1, nx):
        summed = summed + from_x[step - 1]
    from_y[0] = summed

    def y_copy(step):
        other, device = y_peer(step)
        return remote(from_y.at[0, other], from_y.at[1, step - 1], y_send.at[step - 1], y_recv.at[step - 1], device)

    for step in range(1, ny):
        y_copy(step).start()
    for step in range(1, ny):
        y_copy(step).wait_recv()
    summed = from_y[0, y]
    for step in range(1, ny):
        summed = summed + from_y[1, step - 1]
    from_z[z] = summed

    def z_copy(step):
        spot = from_z.at[z]
        return remote(spot, spot, z_send.at[step - 1], z_recv.at[step - 1], z_peer(step)[1])

    for step in range(1, nz):
        z_copy(step).start()
    for step in range(1, nz):
        z_copy(step).wait_recv()
    summed = from_z[0]
    for other in range(1, nz):
        summed = summed + from_z[other]
    gathered[x, y, 0:piece, :] = (summed * scale).astype(jnp.bfloat16)
    if stored > piece:
        gathered[x, y, piece:stored, :] = jnp.zeros((stored - piece, 128), jnp.bfloat16)

    def gy_copy(step):
        spot = gathered.at[x, y]
        return remote(spot, spot, gy_send.at[step - 1], gy_recv.at[step - 1], y_peer(step)[1])

    for step in range(1, ny):
        gy_copy(step).start()
    for step in range(1, ny):
        gy_copy(step).wait_recv()

    def gx_copy(step):
        spot = gathered.at[x]
        return remote(spot, spot, gx_send.at[step - 1], gx_recv.at[step - 1], x_peer(step)[1])

    for step in range(1, nx):
        gx_copy(step).start()
    for step in range(1, nx):
        gx_copy(step).wait_recv()

    for px, py, low, high, source, target, first, last, lane in pieces:
        if source is not None:
            target[first:last, lane:lane + 128] = gathered[px, py, 0:piece, :].astype(jnp.float32)[low:high, :]

    for step in range(1, nx):
        x_copy(step).wait_send()
        gx_copy(step).wait_send()
    for step in range(1, ny):
        y_copy(step).wait_send()
        gy_copy(step).wait_send()
    for step in range(1, nz):
        z_copy(step).wait_send()


def weight_totals(joining, point, depth, scale, strip_count):
    nx, nz, ny = strip_layout(strip_count)
    piece = -(-1600 // (nx * ny) // 8) * 8
    stored = -(-piece // 16) * 16
    vmem = pl.BlockSpec(memory_space=pltpu.VMEM)
    dma = pltpu.SemaphoreType.DMA
    depth_shape = (16, depth.shape[0] * 128)
    shapes = [joining.shape, point.shape, depth_shape]
    a, b, c = pl.pallas_call(
        functools.partial(total_kernel, (nx, nz, ny), piece, stored, scale),
        name="weight_totals",
        out_shape=tuple(jax.ShapeDtypeStruct(shape, jnp.float32) for shape in shapes),
        in_specs=[vmem] * 3,
        out_specs=(vmem,) * 3,
        scratch_shapes=[
            pltpu.VMEM(depth_shape, jnp.float32),
            pltpu.VMEM((nx, ny, piece, 128), jnp.float32),
            pltpu.VMEM((max(nx - 1, 1), ny, piece, 128), jnp.float32),
            pltpu.VMEM((2, ny, piece, 128), jnp.float32),
            pltpu.VMEM((nz, piece, 128), jnp.float32),
            pltpu.VMEM((nx, ny, stored, 128), jnp.bfloat16),
            dma((nx,)), dma((nx,)), dma((ny,)), dma((ny,)), dma((nz,)), dma((nz,)),
            dma((ny,)), dma((ny,)), dma((nx,)), dma((nx,)),
        ],
        compiler_params=pltpu.CompilerParams(
            collective_id=1, has_side_effects=True, vmem_limit_bytes=32 << 20
        ),
    )(joining, point, depth)
    return a, b, c[: depth.shape[1]]


def per_device(features, cotangent, depth_weight, point_weight, joining_weight, branch_mask):
    row_count, col_count, chan_count = features.shape
    strip_count = lax.axis_size("strip")
    local_branch = lax.axis_index("branch")
    pixel_scale = 1.0 / math.sqrt(row_count * col_count * strip_count)
    active = jnp.sum(
        jnp.where(jnp.arange(branch_mask.shape[0]) == local_branch, branch_mask, 0)
    ).astype(jnp.float32)
    active = jnp.full((1, point_weight.shape[2]), active)
    output, joining_part, point_part, depth_part = branch_step(
        features, cotangent, depth_weight[0], point_weight[0], joining_weight, active, strip_count
    )
    joining_total, point_total, depth_total = weight_totals(
        joining_part, point_part, depth_part, pixel_scale, strip_count
    )
    return (output, joining_total, point_total[None], depth_total[None])


def solution(mesh):
    placed = (
        P("strip", None, None),
        P("strip", None, "branch"),
        P("branch", None, None),
        P("branch", None, None),
        P("branch", None),
        P(),
    )
    return jax.shard_map(
        per_device,
        mesh=mesh,
        in_specs=placed,
        out_specs=(
            P("strip", None, "branch"),
            P("branch", None),
            P("branch", None, None),
            P("branch", None, None),
        ),
        check_vma=False,
    )
```

time: 165 us -> 143 us (0.87)
  the two profiles are of different devices: /device:TPU:4 before, /device:TPU:1 now
where the time goes in v2:
time: 143 us; the launch traced here: 141 us
  Pallas kernels  132 us (92%)
  local copies, waits for them, and re-layouts  6.13 us (4%)
  other arithmetic  1.56 us (1%)
    pallas_call x1, Pallas kernels, branch_step(): pl.pallas_call(functools.partial(branch_kernel, strip_count), name='branc...  90.4 us
    pallas_call x1, Pallas kernels, weight_totals(): pl.pallas_call(functools.partial(total_kernel, (nx, nz, ny), piece, store...  41.4 us
    unnamed x11, local copies, waits for them, and re-layouts  3.44 us

profile of v2, /device:TPU:1, one launch (start us, length us, event | category | flops | bytes accessed | tf_op | source)
XLA Modules:
  0.0 140.8 jit_solution(9818656806880145923)
XLA Ops:
  0.6 0.0 copy-start.1
  0.6 0.0 copy-start
  0.7 1.3 fusion
  2.7 0.7 reshape.12
  3.4 0.9 slice.39
  4.3 0.2 copy.23
  4.5 0.9 fusion.1
  5.4 0.1 copy.21
  5.5 0.1 copy.22
  5.7 0.1 pad_maximum_fusion.1.cot
  5.8 0.0 copy-done.1
  5.8 0.0 copy-done
  5.8 90.4 %branch_step.1 = (bf16[4,192,128]{2,1,0:T(8,128)(2,1)S(1)}, f32[256,256]{1,0:T(8,128)S(1)}, f32[512,256]{1,0:T(8,128)S(1)}, f32[4,9,8,128]{3,2,1,0:T(8,128)S(1)}) custom-call(bf16[8,192,512]{2,1,0:T(8,128)(2,1)} %feat.1, bf16[4,192,128]{2,1,0:T(8,128)(2,1)S(1)} %pad_maximum_fusion.1.cot, f32[4,9,128]{2,1,0:T(8,128)S(1)} %bitcast.9, ...), custom_call_target="tpu_custom_call" | custom-call | tf_op jit(solution)/shard_map/branch_step/pallas_call | solution.py:341
  96.2 41.4 %weight_totals.1 = (f32[256,256]{1,0:T(8,128)S(1)}, f32[512,256]{1,0:T(8,128)S(1)}, f32[16,512]{1,0:T(8,128)S(1)}) custom-call(f32[256,256]{1,0:T(8,128)S(1)} %get-tuple-element.12.joining, f32[512,256]{1,0:T(8,128)S(1)} %get-tuple-element.13.point, f32[4,9,8,128]{3,2,1,0:T(8,128)S(1)} %get-tuple-element.14.depth), custom_call_target="tpu_custom_call" | custom-call | tf_op jit(solution)/shard_map/weight_totals/pallas_call | solution.py:530
  137.6 0.6 copy.20
  138.2 0.1 slice.42
  138.3 0.1 pad_maximum_fusion
  138.4 0.9 copy.19
  139.3 0.7 copy.28
  140.0 0.8 copy.29
  (4 shorter events, 0.0 us)
Async XLA Ops:
  0.6 5.2 %copy-start.1 = (bf16[256,256]{1,0:T(8,128)(2,1)S(1)}, bf16[256,256]{1,0:T(8,128)(2,1)}, u32[]{:S(2)}) copy-start(bf16[256,256]{1,0:T(8,128)(2,1)} %join_w.1) | copy-start | bytes 393220
  0.6 5.2 %copy-start = (bf16[1,512,256]{2,1,0:T(8,128)(2,1)S(1)}, bf16[1,512,256]{2,1,0:T(8,128)(2,1)}, u32[]{:S(2)}) copy-start(bf16[1,512,256]{2,1,0:T(8,128)(2,1)} %param.9) | copy-start | bytes 786436

commit v3 on v2

--- a/solution.py
+++ b/solution.py
@@ -42,8 +42,8 @@
 
 
 CHUNKS = 4
-LOW_ROWS = (2, 3, 0, 1)
-HIGH_ROWS = (4, 5, 6, 7)
+LOW_ROWS = (2, 0, 3, 1)
+HIGH_ROWS = (4, 6, 5, 7)
 EDGE = 24
 
 
@@ -57,7 +57,7 @@
 
 
 def branch_kernel(
-    strip_count, feat, cot, depth_w, point_w, join_w, active, out, join_part, point_part, depth_part,
+    strip_count, feat, cot, depth_w, point_w, join_w, mask, out, join_part, point_part, depth_part,
     ext, taps, dw_out, slope, branch_out, blocks, near, away, far, total, grads, grad_dw,
     own_sem, send, recv, pass_send, pass_recv,
     near_send, near_recv, far_send, far_recv, gfar_send, gfar_recv, gnear_send, gnear_recv,
@@ -77,6 +77,7 @@
     across = (strip, other)
     after = (lax.rem(strip + 1, strip_count), branch)
     before = (lax.rem(strip + strip_count - 1, strip_count), branch)
+    active = mask[branch].astype(jnp.float32)
     greet(pltpu.get_barrier_semaphore(), [after, before, sibling, across])
 
     def remote(source, target, send_sem, recv_sem, device):
@@ -112,13 +113,16 @@
         return remote(spot, spot, pass_send.at[at, step, line], pass_recv.at[at, step, line], sibling)
 
     ways = (1, -1)
-    for line in range(half):
+
+    def send_own(line):
         for way in ways:
 
             @pl.when(exists(way))
             def _():
                 link_copy(way, 0, line).start()
 
+    send_own(0)
+    send_own(1)
     own = pltpu.make_async_copy(feat, ext.at[pl.ds(centre, rows)], own_sem)
     own.start()
 
@@ -210,22 +214,22 @@
             widen(row, 2)
 
             def depthwise(tile, carry):
+                lanes = pl.ds(pl.multiple_of(tile * 128, 128), 128)
+                weights = depth_w[0, :, lanes].astype(jnp.float32)
                 summed = jnp.zeros((cols, 128), jnp.float32)
                 for part in range(9):
                     piece = taps[row, part // 3, tile, tap_columns(part % 3), :]
-                    summed = summed + piece * depth_w[tile, part:part + 1, :]
-                dw_out[chunk, place * cols:(place + 1) * cols, pl.ds(pl.multiple_of(tile * 128, 128), 128)] = (
-                    summed.astype(jnp.bfloat16)
-                )
+                    summed = summed + piece * weights[part:part + 1, :]
+                dw_out[chunk, place * cols:(place + 1) * cols, lanes] = summed.astype(jnp.bfloat16)
                 return carry
 
             lax.fori_loop(0, tiles, depthwise, 0)
-        pre = jnp.dot(dw_out[chunk], point_w[...], preferred_element_type=jnp.float32)
+        pre = jnp.dot(dw_out[chunk], point_w[0], preferred_element_type=jnp.float32)
         inner = jnp.tanh(tanh_coef * (pre + cubic_coef * pre * pre * pre))
         slope[chunk] = 0.5 * (1.0 + inner) + 0.5 * pre * (1.0 - inner * inner) * tanh_coef * (
             1.0 + slope_coef * pre * pre
         )
-        branch_out[chunk] = (0.5 * pre * (1.0 + inner) * active[...]).astype(jnp.bfloat16)
+        branch_out[chunk] = (0.5 * pre * (1.0 + inner) * active).astype(jnp.bfloat16)
         part_sum = jnp.dot(branch_out[chunk], join_w[...], preferred_element_type=jnp.float32)
         for pair in range(2):
             lanes = slice(128 * pair, 128 * (pair + 1))
@@ -252,10 +256,14 @@
         rise = 0.5 * (1.0 + inner) + 0.5 * joined * (1.0 - inner * inner) * tanh_coef * (
             1.0 + slope_coef * joined * joined
         )
-        grads[branch, chunk] = (cot[chunk].astype(jnp.float32) * rise).astype(jnp.bfloat16)
+        low_row, high_row = LOW_ROWS[chunk], HIGH_ROWS[chunk]
+        given = jnp.concatenate([cot[low_row].astype(jnp.float32), cot[high_row].astype(jnp.float32)], axis=1)
+        grads[branch, chunk] = (given * rise).astype(jnp.bfloat16)
         grad_far(chunk).start()
         grad_near(chunk, 0, branch).start()
-        out[chunk] = (0.5 * joined * (1.0 + inner)).astype(out.dtype)
+        result = (0.5 * joined * (1.0 + inner)).astype(out.dtype)
+        out[low_row] = result[:, :64]
+        out[high_row] = result[:, 64:]
 
     def hand_on(chunk):
         grad_far(chunk).wait_recv()
@@ -274,9 +282,9 @@
         full_grad = jnp.concatenate(
             [jnp.concatenate(low_parts, axis=1), jnp.concatenate(high_parts, axis=1)], axis=0
         ).astype(jnp.bfloat16)
-        grad_branch = contract_cols(full_grad, join_w[...]) * active[...]
+        grad_branch = contract_cols(full_grad, join_w[...]) * active
         grad_pre = (grad_branch * slope[chunk]).astype(jnp.bfloat16)
-        grad_dw[...] = contract_cols(grad_pre, point_w[...])
+        grad_dw[...] = contract_cols(grad_pre, point_w[0])
         join_part[...] += contract_rows(branch_out[chunk], full_grad)
         point_part[...] += contract_rows(dw_out[chunk], grad_pre)
         for place, row in ((0, LOW_ROWS[chunk]), (1, HIGH_ROWS[chunk])):
@@ -291,17 +299,40 @@
             lax.fori_loop(0, tiles, depth_sums, 0)
 
     for step in range(HOPS - 1):
-        for line in range(half):
+        for line in (0, 1):
             arrive(step, line)
+    send_own(2)
+    send_own(3)
     for step in range(HOPS - 1):
-        for line in range(half):
+        for line in (0, 1):
             passed(step, line)
-
-    stages = (forward, pair_sum, finish_sum, hand_on, backward)
-    for turn in range(CHUNKS + len(stages) - 1):
-        for index, stage in enumerate(stages):
-            if 0 <= turn - index < CHUNKS:
-                stage(turn - index)
+    forward(0)
+    pair_sum(0)
+    forward(1)
+    finish_sum(0)
+    pair_sum(1)
+    arrive(0, 2)
+    hand_on(0)
+    finish_sum(1)
+    arrive(0, 3)
+    backward(0)
+    hand_on(1)
+    arrive(1, 2)
+    backward(1)
+    arrive(1, 3)
+    for step in range(HOPS - 1):
+        for line in (2, 3):
+            passed(step, line)
+    forward(2)
+    pair_sum(2)
+    forward(3)
+    finish_sum(2)
+    pair_sum(3)
+    hand_on(2)
+    finish_sum(3)
+    backward(2)
+    hand_on(3)
+    backward(3)
 
     for step in range(HOPS):
         for line in range(half):
@@ -324,30 +355,24 @@
         grad_near(chunk, 1, other).wait_send()
 
 
-def branch_step(features, cotangent, depth_weight, point_weight, joining_weight, active, strip_count):
+def branch_step(features, cotangent, depth_weight, point_weight, joining_weight, branch_mask, strip_count):
     rows, cols, chans = features.shape
-    width = point_weight.shape[1]
+    width = point_weight.shape[2]
     half = rows // 2
     tiles = chans // 128
-
-    def lines(array, order):
-        return jnp.concatenate([array[row:row + 1] for row in order], 0)
-
-    packed = jnp.concatenate([lines(cotangent, LOW_ROWS), lines(cotangent, HIGH_ROWS)], axis=2)
-    taps_weight = depth_weight.astype(jnp.float32).reshape(9, tiles, 128).transpose(1, 0, 2)
     vmem = pl.BlockSpec(memory_space=pltpu.VMEM)
     dma = pltpu.SemaphoreType.DMA
     low, wide = jnp.bfloat16, jnp.float32
-    out, join_part, point_part, depth_part = pl.pallas_call(
+    return pl.pallas_call(
         functools.partial(branch_kernel, strip_count),
         name="branch_step",
         out_shape=(
-            jax.ShapeDtypeStruct((CHUNKS, cols, 128), low),
+            jax.ShapeDtypeStruct(cotangent.shape, low),
             jax.ShapeDtypeStruct((width, width), wide),
             jax.ShapeDtypeStruct((chans, width), wide),
             jax.ShapeDtypeStruct((tiles, 9, 8, 128), wide),
         ),
-        in_specs=[pl.BlockSpec(memory_space=pl.ANY)] + [vmem] * 5,
+        in_specs=[pl.BlockSpec(memory_space=pl.ANY)] + [vmem] * 4 + [pl.BlockSpec(memory_space=pltpu.SMEM)],
         out_specs=(vmem,) * 4,
         scratch_shapes=[
             pltpu.VMEM(((2 * HOPS + 1) * rows, cols, chans), low),
@@ -370,13 +395,7 @@
         compiler_params=pltpu.CompilerParams(
             collective_id=0, has_side_effects=True, vmem_limit_bytes=52 << 20
         ),
-    )(features, packed, taps_weight, point_weight, joining_weight, active)
-    by_row = {}
-    for chunk in range(CHUNKS):
-        by_row[LOW_ROWS[chunk]] = out[chunk:chunk + 1, :, :64]
-        by_row[HIGH_ROWS[chunk]] = out[chunk:chunk + 1, :, 64:]
-    output = jnp.concatenate([by_row[row] for row in range(rows)], 0)
-    return output, join_part, point_part, depth_part
+    )(features, cotangent, depth_weight, point_weight, joining_weight, branch_mask)
 
 
 def total_kernel(
@@ -553,14 +572,9 @@
 def per_device(features, cotangent, depth_weight, point_weight, joining_weight, branch_mask):
     row_count, col_count, chan_count = features.shape
     strip_count = lax.axis_size("strip")
-    local_branch = lax.axis_index("branch")
     pixel_scale = 1.0 / math.sqrt(row_count * col_count * strip_count)
-    active = jnp.sum(
-        jnp.where(jnp.arange(branch_mask.shape[0]) == local_branch, branch_mask, 0)
-    ).astype(jnp.float32)
-    active = jnp.full((1, point_weight.shape[2]), active)
     output, joining_part, point_part, depth_part = branch_step(
-        features, cotangent, depth_weight[0], point_weight[0], joining_weight, active, strip_count
+        features, cotangent, depth_weight, point_weight, joining_weight, branch_mask, strip_count
     )
     joining_total, point_total, depth_total = weight_totals(
         joining_part, point_part, depth_part, pixel_scale, strip_count

time: 143 us -> 166 us (1.16)
  Pallas kernels: 132 us -> 156 us
  local copies, waits for them, and re-layouts: 6.13 us -> 8.45 us
    pallas_call x1, Pallas kernels: 90.4 us -> 115 us  [branch_step(): pl.pallas_call(functools.partial(branch_kernel, strip_count), name='branc...]
    unnamed x11 -> x15, local copies, waits for them, and re-layouts: 3.44 us -> 8.45 us
    slice x4 -> x0, local copies, waits for them, and re-layouts: 1.94 us -> none  [the longest x2 1.81 us: lines(): return jnp.concatenate([array[row:row + 1] for row in order], 0)]
where the time goes in v3:
time: 166 us; the launch traced here: 165 us
  Pallas kernels  156 us (94%)
  local copies, waits for them, and re-layouts  8.45 us (5%)
    pallas_call x1, Pallas kernels, branch_step(): pl.pallas_call(functools.partial(branch_kernel, strip_count), name='branc...  115 us
    pallas_call x1, Pallas kernels, weight_totals(): pl.pallas_call(functools.partial(total_kernel, (nx, nz, ny), piece, store...  41.5 us
    unnamed x15, local copies, waits for them, and re-layouts  8.45 us

profile of v3, /device:TPU:1, one launch (start us, length us, event | category | flops | bytes accessed | tf_op | source)
XLA Modules:
  0.0 165.4 jit_solution(8317388474580978282)
XLA Ops:
  0.6 1.2 copy.10.cot
  1.8 0.0 copy-start.1
  1.8 0.9 copy-done.1
  2.8 0.0 copy-start.2
  2.8 0.9 copy-done.2
  3.7 0.0 copy-start.3
  3.7 0.7 copy-done.3
  4.4 0.0 copy-start.4
  4.4 0.7 copy-done.4
  5.0 114.8 %branch_step.1 = (bf16[8,192,64]{2,1,0:T(8,128)(2,1)S(1)}, f32[256,256]{1,0:T(8,128)S(1)}, f32[512,256]{1,0:T(8,128)}, f32[4,9,8,128]{3,2,1,0:T(8,128)S(1)}) custom-call(bf16[8,192,512]{2,1,0:T(8,128)(2,1)} %feat.1, bf16[8,192,64]{2,1,0:T(8,128)(2,1)S(1)} %copy.10.cot, bf16[1,9,512]{2,1,0:T(8,128)(2,1)S(1)} %copy-done.3, bf16[1,512,256]{2,1,0:T(8,128)(2,1)S(1)} %copy-done.1, ...), custom_call_target="tpu_custom_call" | custom-call | tf_op jit(solution)/shard_map/branch_step/pallas_call | solution.py:366
  119.9 0.9 copy.11
  120.8 0.0 copy-start
  120.8 1.0 copy-done
  121.8 41.5 %weight_totals.1 = (f32[256,256]{1,0:T(8,128)S(1)}, f32[512,256]{1,0:T(8,128)S(1)}, f32[16,512]{1,0:T(8,128)S(1)}) custom-call(f32[256,256]{1,0:T(8,128)S(1)} %get-tuple-element.12.joining, f32[512,256]{1,0:T(8,128)S(1)} %copy-done, f32[4,9,8,128]{3,2,1,0:T(8,128)S(1)} %get-tuple-element.14.depth), custom_call_target="tpu_custom_call" | custom-call | tf_op jit(solution)/shard_map/weight_totals/pallas_call | solution.py:549
  163.3 0.6 copy.12
  163.9 0.7 copy.15
  164.6 0.8 copy.16
  (1 shorter events, 0.0 us)
Async XLA Ops:
  1.8 1.0 copy-start.1
  2.8 0.9 copy-start.2
  3.7 0.7 copy-start.3
  4.4 0.7 copy-start.4
  120.8 1.0 copy-start

commit v4 on v3

--- a/solution.py
+++ b/solution.py
@@ -42,8 +42,8 @@
 
 
 CHUNKS = 4
-LOW_ROWS = (2, 0, 3, 1)
-HIGH_ROWS = (4, 6, 5, 7)
+LOW_ROWS = (2, 3, 0, 1)
+HIGH_ROWS = (4, 5, 6, 7)
 EDGE = 24
 
 
@@ -121,8 +121,8 @@
             def _():
                 link_copy(way, 0, line).start()
 
-    send_own(0)
-    send_own(1)
+    for line in range(half):
+        send_own(line)
     own = pltpu.make_async_copy(feat, ext.at[pl.ds(centre, rows)], own_sem)
     own.start()
 
@@ -299,40 +299,17 @@
             lax.fori_loop(0, tiles, depth_sums, 0)
 
     for step in range(HOPS - 1):
-        for line in (0, 1):
+        for line in range(half):
             arrive(step, line)
-    send_own(2)
-    send_own(3)
     for step in range(HOPS - 1):
-        for line in (0, 1):
+        for line in range(half):
             passed(step, line)
-    forward(0)
-    pair_sum(0)
-    forward(1)
-    finish_sum(0)
-    pair_sum(1)
-    arrive(0, 2)
-    hand_on(0)
-    finish_sum(1)
-    arrive(0, 3)
-    backward(0)
-    hand_on(1)
-    arrive(1, 2)
-    backward(1)
-    arrive(1, 3)
-    for step in range(HOPS - 1):
-        for line in (2, 3):
-            passed(step, line)
-    forward(2)
-    pair_sum(2)
-    forward(3)
-    finish_sum(2)
-    pair_sum(3)
-    hand_on(2)
-    finish_sum(3)
-    backward(2)
-    hand_on(3)
-    backward(3)
+
+    stages = (forward, pair_sum, finish_sum, hand_on, backward)
+    for turn in range(CHUNKS + len(stages) - 1):
+        for index, stage in enumerate(stages):
+            if 0 <= turn - index < CHUNKS:
+                stage(turn - index)
 
     for step in range(HOPS):
         for line in range(half):
@@ -400,7 +377,7 @@
 
 def total_kernel(
     layout, piece, stored, scale, joining, point, depth, joining_out, point_out, depth_out,
-    depth_rows, mine, from_x, from_y, from_z, gathered,
+    depth_rows, mine, sent, from_x, from_y, from_z, gathered,
     x_send, x_recv, y_send, y_recv, z_send, z_recv, gy_send, gy_recv, gx_send, gx_recv,
 ):
     nx, nz, ny = layout
@@ -465,9 +442,15 @@
         else:
             mine[px, py, low:high, :] = source[first:last, lane:lane + 128]
 
+    for px in range(nx):
+        for py in range(ny):
+            sent[px, py, 0:piece, :] = mine[px, py].astype(jnp.bfloat16)
+            if stored > piece:
+                sent[px, py, piece:stored, :] = jnp.zeros((stored - piece, 128), jnp.bfloat16)
+
     def x_copy(step):
         other, device = x_peer(step)
-        return remote(mine.at[other], from_x.at[step - 1], x_send.at[step - 1], x_recv.at[step - 1], device)
+        return remote(sent.at[other], from_x.at[step - 1], x_send.at[step - 1], x_recv.at[step - 1], device)
 
     for step in range(1, nx):
         x_copy(step).start()
@@ -475,8 +458,12 @@
         x_copy(step).wait_recv()
     summed = mine[x]
     for step in range(1, nx):
-        summed = summed + from_x[step - 1]
-    from_y[0] = summed
+        summed = summed + from_x[step - 1].astype(jnp.float32)[:, 0:piece, :]
+    mine[0] = summed
+    for py in range(ny):
+        from_y[0, py, 0:piece, :] = mine[0, py].astype(jnp.bfloat16)
+        if stored > piece:
+            from_y[0, py, piece:stored, :] = jnp.zeros((stored - piece, 128), jnp.bfloat16)
 
     def y_copy(step):
         other, device = y_peer(step)
@@ -486,9 +473,9 @@
         y_copy(step).start()
     for step in range(1, ny):
         y_copy(step).wait_recv()
-    summed = from_y[0, y]
+    summed = mine[0, y]
     for step in range(1, ny):
-        summed = summed + from_y[1, step - 1]
+        summed = summed + from_y[1, step - 1].astype(jnp.float32)[0:piece, :]
     from_z[z] = summed
 
     def z_copy(step):
@@ -555,8 +542,9 @@
         scratch_shapes=[
             pltpu.VMEM(depth_shape, jnp.float32),
             pltpu.VMEM((nx, ny, piece, 128), jnp.float32),
-            pltpu.VMEM((max(nx - 1, 1), ny, piece, 128), jnp.float32),
-            pltpu.VMEM((2, ny, piece, 128), jnp.float32),
+            pltpu.VMEM((nx, ny, stored, 128), jnp.bfloat16),
+            pltpu.VMEM((max(nx - 1, 1), ny, stored, 128), jnp.bfloat16),
+            pltpu.VMEM((2, ny, stored, 128), jnp.bfloat16),
             pltpu.VMEM((nz, piece, 128), jnp.float32),
             pltpu.VMEM((nx, ny, stored, 128), jnp.bfloat16),
             dma((nx,)), dma((nx,)), dma((ny,)), dma((ny,)), dma((nz,)), dma((nz,)),

time: 166 us -> 138 us (0.83); the launches traced: 165 us -> 135 us
  Pallas kernels: 156 us -> 126 us
    pallas_call x1, Pallas kernels: 115 us -> 92.1 us  [branch_step(): pl.pallas_call(functools.partial(branch_kernel, strip_count), name='branc...]
    pallas_call x1, Pallas kernels: 41.5 us -> 33.9 us  [weight_totals(): pl.pallas_call(functools.partial(total_kernel, (nx, nz, ny), piece, store...]
where the time goes in v4:
time: 138 us; the launch traced here: 135 us
  Pallas kernels  126 us (91%)
  local copies, waits for them, and re-layouts  8.45 us (6%)
    pallas_call x1, Pallas kernels, branch_step(): pl.pallas_call(functools.partial(branch_kernel, strip_count), name='branc...  92.1 us
    pallas_call x1, Pallas kernels, weight_totals(): pl.pallas_call(functools.partial(total_kernel, (nx, nz, ny), piece, store...  33.9 us
    unnamed x15, local copies, waits for them, and re-layouts  8.45 us

profile of v4, /device:TPU:1, one launch (start us, length us, event | category | flops | bytes accessed | tf_op | source)
XLA Modules:
  0.0 135.1 jit_solution(6351945120378064366)
XLA Ops:
  0.6 1.2 copy.10.cot
  1.8 0.0 copy-start.1
  1.8 0.9 copy-done.1
  2.8 0.0 copy-start.2
  2.8 0.9 copy-done.2
  3.7 0.0 copy-start.3
  3.7 0.7 copy-done.3
  4.4 0.0 copy-start.4
  4.4 0.7 copy-done.4
  5.0 92.1 %branch_step.1 = (bf16[8,192,64]{2,1,0:T(8,128)(2,1)S(1)}, f32[256,256]{1,0:T(8,128)S(1)}, f32[512,256]{1,0:T(8,128)}, f32[4,9,8,128]{3,2,1,0:T(8,128)S(1)}) custom-call(bf16[8,192,512]{2,1,0:T(8,128)(2,1)} %feat.1, bf16[8,192,64]{2,1,0:T(8,128)(2,1)S(1)} %copy.10.cot, bf16[1,9,512]{2,1,0:T(8,128)(2,1)S(1)} %copy-done.3, bf16[1,512,256]{2,1,0:T(8,128)(2,1)S(1)} %copy-done.1, ...), custom_call_target="tpu_custom_call" | custom-call | tf_op jit(solution)/shard_map/branch_step/pallas_call | solution.py:343
  97.1 0.9 copy.11
  98.0 0.0 copy-start
  98.0 1.0 copy-done
  99.1 33.9 %weight_totals.1 = (f32[256,256]{1,0:T(8,128)S(1)}, f32[512,256]{1,0:T(8,128)S(1)}, f32[16,512]{1,0:T(8,128)S(1)}) custom-call(f32[256,256]{1,0:T(8,128)S(1)} %get-tuple-element.12.joining, f32[512,256]{1,0:T(8,128)S(1)} %copy-done, f32[4,9,8,128]{3,2,1,0:T(8,128)S(1)} %get-tuple-element.14.depth), custom_call_target="tpu_custom_call" | custom-call | tf_op jit(solution)/shard_map/weight_totals/pallas_call | solution.py:536
  132.9 0.6 copy.12
  133.6 0.7 copy.15
  134.3 0.8 copy.16
  (1 shorter events, 0.0 us)
Async XLA Ops:
  1.8 1.0 copy-start.1
  2.8 0.9 copy-start.2
  3.7 0.7 copy-start.3
  4.4 0.7 copy-start.4
  98.0 1.0 copy-start

commit v5 on v4

--- a/solution.py
+++ b/solution.py
@@ -442,17 +442,16 @@
         else:
             mine[px, py, low:high, :] = source[first:last, lane:lane + 128]
 
-    for px in range(nx):
+    def x_copy(step):
+        other, device = x_peer(step)
+        return remote(sent.at[other], from_x.at[step - 1], x_send.at[step - 1], x_recv.at[step - 1], device)
+
+    for step in range(1, nx):
+        px = x_peer(step)[0]
         for py in range(ny):
             sent[px, py, 0:piece, :] = mine[px, py].astype(jnp.bfloat16)
             if stored > piece:
                 sent[px, py, piece:stored, :] = jnp.zeros((stored - piece, 128), jnp.bfloat16)
-
-    def x_copy(step):
-        other, device = x_peer(step)
-        return remote(sent.at[other], from_x.at[step - 1], x_send.at[step - 1], x_recv.at[step - 1], device)
-
-    for step in range(1, nx):
         x_copy(step).start()
     for step in range(1, nx):
         x_copy(step).wait_recv()
@@ -476,7 +475,9 @@
     summed = mine[0, y]
     for step in range(1, ny):
         summed = summed + from_y[1, step - 1].astype(jnp.float32)[0:piece, :]
-    from_z[z] = summed
+    from_z[z, 0:piece, :] = summed.astype(jnp.bfloat16)
+    if stored > piece:
+        from_z[z, piece:stored, :] = jnp.zeros((stored - piece, 128), jnp.bfloat16)
 
     def z_copy(step):
         spot = from_z.at[z]
@@ -486,9 +487,9 @@
         z_copy(step).start()
     for step in range(1, nz):
         z_copy(step).wait_recv()
-    summed = from_z[0]
+    summed = from_z[0].astype(jnp.float32)[0:piece, :]
     for other in range(1, nz):
-        summed = summed + from_z[other]
+        summed = summed + from_z[other].astype(jnp.float32)[0:piece, :]
     gathered[x, y, 0:piece, :] = (summed * scale).astype(jnp.bfloat16)
     if stored > piece:
         gathered[x, y, piece:stored, :] = jnp.zeros((stored - piece, 128), jnp.bfloat16)
@@ -545,7 +546,7 @@
             pltpu.VMEM((nx, ny, stored, 128), jnp.bfloat16),
             pltpu.VMEM((max(nx - 1, 1), ny, stored, 128), jnp.bfloat16),
             pltpu.VMEM((2, ny, stored, 128), jnp.bfloat16),
-            pltpu.VMEM((nz, piece, 128), jnp.float32),
+            pltpu.VMEM((nz, stored, 128), jnp.bfloat16),
             pltpu.VMEM((nx, ny, stored, 128), jnp.bfloat16),
             dma((nx,)), dma((nx,)), dma((ny,)), dma((ny,)), dma((nz,)), dma((nz,)),
             dma((ny,)), dma((ny,)), dma((nx,)), dma((nx,)),

time: 138 us -> 137 us (level)
  no operation moved by 1% of the time
where the time goes in v5:
time: 137 us; the launch traced here: 135 us
  Pallas kernels  126 us (92%)
  local copies, waits for them, and re-layouts  8.45 us (6%)
    pallas_call x1, Pallas kernels, branch_step(): pl.pallas_call(functools.partial(branch_kernel, strip_count), name='branc...  92.1 us
    pallas_call x1, Pallas kernels, weight_totals(): pl.pallas_call(functools.partial(total_kernel, (nx, nz, ny), piece, store...  33.6 us
    unnamed x15, local copies, waits for them, and re-layouts  8.45 us

profile of v5, /device:TPU:1, one launch (start us, length us, event | category | flops | bytes accessed | tf_op | source)
XLA Modules:
  0.0 134.8 jit_solution(10324619660548996786)
XLA Ops:
  0.6 1.2 copy.10.cot
  1.8 0.0 copy-start.1
  1.8 0.9 copy-done.1
  2.8 0.0 copy-start.2
  2.8 0.9 copy-done.2
  3.7 0.0 copy-start.3
  3.7 0.7 copy-done.3
  4.4 0.0 copy-start.4
  4.4 0.7 copy-done.4
  5.0 92.1 %branch_step.1 = (bf16[8,192,64]{2,1,0:T(8,128)(2,1)S(1)}, f32[256,256]{1,0:T(8,128)S(1)}, f32[512,256]{1,0:T(8,128)}, f32[4,9,8,128]{3,2,1,0:T(8,128)S(1)}) custom-call(bf16[8,192,512]{2,1,0:T(8,128)(2,1)} %feat.1, bf16[8,192,64]{2,1,0:T(8,128)(2,1)S(1)} %copy.10.cot, bf16[1,9,512]{2,1,0:T(8,128)(2,1)S(1)} %copy-done.3, bf16[1,512,256]{2,1,0:T(8,128)(2,1)S(1)} %copy-done.1, ...), custom_call_target="tpu_custom_call" | custom-call | tf_op jit(solution)/shard_map/branch_step/pallas_call | solution.py:343
  97.1 0.9 copy.11
  98.0 0.0 copy-start
  98.0 1.0 copy-done
  99.1 33.6 %weight_totals.1 = (f32[256,256]{1,0:T(8,128)S(1)}, f32[512,256]{1,0:T(8,128)S(1)}, f32[16,512]{1,0:T(8,128)S(1)}) custom-call(f32[256,256]{1,0:T(8,128)S(1)} %get-tuple-element.12.joining, f32[512,256]{1,0:T(8,128)S(1)} %copy-done, f32[4,9,8,128]{3,2,1,0:T(8,128)S(1)} %get-tuple-element.14.depth), custom_call_target="tpu_custom_call" | custom-call | tf_op jit(solution)/shard_map/weight_totals/pallas_call | solution.py:537
  132.7 0.6 copy.12
  133.3 0.7 copy.15
  134.0 0.8 copy.16
  (1 shorter events, 0.0 us)
Async XLA Ops:
  1.8 1.0 copy-start.1
  2.8 0.9 copy-start.2
  3.7 0.7 copy-start.3
  4.4 0.7 copy-start.4
  98.0 1.0 copy-start
